TPU v7x, 256 devices: a whole 4x4x8 slice. The times are simulated.
256 devices in a mesh: bead: 32 (over x, y, core), wave: 4 (over z_hi), grp: 2 (over z_lo).
Axes of the slice: x: 4, y: 4, z: 8 (z_hi: 4, z_lo: 2; z = z_hi * 2 + z_lo), core: 2. Of those that a mesh axis runs over, the one named last changes fastest.
Arguments:
- features: float32 [32768, 512], P(('bead', 'wave', 'grp')), may hold values from -6 to 6
- positions: float32 [3, 32768], P(None, ('bead', 'wave', 'grp')), may hold values from 0 to 1
- wavevectors: int32 [3, 4096], P(None, ('wave', 'grp')), may hold values from -6 to 6
- neighbour_slots: int32 [32, 32768], P(None, ('bead', 'wave', 'grp')), may hold values from 0 to 383
- neighbour_count: int32 [32768], P(('bead', 'wave', 'grp')), may hold values from 8 to 32
- pair_distance: float32 [32, 32768], P(None, ('bead', 'wave', 'grp')), may hold values from 0.3 to 2.4
- w_self: float32 [512, 512], replicated, may hold values from -0.25 to 0.25
- w_neighbour: float32 [512, 512], replicated, may hold values from -0.25 to 0.25
- w_edge: float32 [16, 512], replicated, may hold values from -1.5 to 1.5
- w_message: float32 [512, 512], replicated, may hold values from -0.25 to 0.25
- spec_filter: float32 [4096, 512], P(('wave', 'grp')), may hold values from -4 to 4
- norm_gain: float32 [512], replicated, may hold values from 0.5 to 1.5
- w_up: float32 [512, 512], replicated, may hold values from -0.25 to 0.25
- w_down: float32 [512, 512], replicated, may hold values from -0.25 to 0.25
Outputs:
- updated: float32 [32768, 512], P(('bead', 'wave', 'grp'))
All inputs are finite; a program needn't handle non-finite values.
Results may differ from a plain program's by a relative error of at most 0.0003.
Values sent between devices are 32-bit elements; how exact they have to be, the bound alone decides.
No kernel may reach another device: no remote copies, remote signals or barrier semaphores. Data moves between devices by JAX's collectives and lax.ppermute only.
A program may use at most 128 MiB of HBM per device.

v0:
```python
import functools

import jax
import jax.numpy as jnp
from jax import lax
from jax.experimental import pallas as pl
from jax.experimental.pallas import tpu as pltpu
from jax.sharding import Mesh, PartitionSpec as P

KVEC = 4096
BLOCK = 128
WIDTH = 512
SLOTS = 32
RADIAL = 16
epsilon = 1e-05
reach = 2.5

TRADE = ("core", "zh", "zl")
TOTAL = ("x", "y")
EVERY = ("x", "y", "core", "zh", "zl")
FEATS = 32
AT_POS = 32
AT_VEC = 35
AT_FILTER = 41
ROWS = 48
USED = tuple(range(7)) + tuple(range(9, 15))

SIN = (6.283182792843448, -41.3414193330158, 81.59613740878913, -76.57967400034956,
       41.20368207513971, -12.268761447381701)
COS = (0.9999999890563522, -19.73920449855691, 64.93911741205494, -85.45013861232991,
       60.16762307755092, -25.967568454487537, 6.528613369793176)

bf16 = jnp.bfloat16
f32 = jnp.float32
NT = (((1,), (1,)), ((), ()))


def halves(value):
    high = value.astype(bf16)
    return high, (value - high.astype(f32)).astype(bf16)


def dot(left, right):
    return jnp.dot(left, right, preferred_element_type=f32)


def dot_nt(left, right):
    return lax.dot_general(left, right, NT, preferred_element_type=f32)


def dot3(left, right):
    left_high, left_low = halves(left)
    right_high, right_low = halves(right)
    return dot(left_high, right_high) + (dot(left_high, right_low) + dot(left_low, right_high))


def turn(cycles):
    part = cycles - jnp.round(cycles)
    square = part * part
    cosine = jnp.full_like(square, COS[-1])
    for factor in COS[-2::-1]:
        cosine = cosine * square + factor
    sine = jnp.full_like(square, SIN[-1])
    for factor in SIN[-2::-1]:
        sine = sine * square + factor
    return cosine, sine * part


def whole(count):
    return [pl.BlockSpec(memory_space=pltpu.VMEM)] * count


def call(kernel, outs, ins, scalars=0, scratch=(), flops=0, name=None):
    specs = [pl.BlockSpec(memory_space=pltpu.SMEM)] * scalars + whole(len(ins) - scalars)
    many = isinstance(outs, (tuple, list))
    size = sum(v.size * v.dtype.itemsize for v in ins)
    return pl.pallas_call(
        kernel,
        out_shape=outs,
        in_specs=specs,
        out_specs=tuple(whole(len(outs))) if many else whole(1)[0],
        scratch_shapes=list(scratch),
        compiler_params=pltpu.CompilerParams(vmem_limit_bytes=56 * 1024 * 1024),
        cost_estimate=pl.CostEstimate(flops=flops, bytes_accessed=size, transcendentals=0),
        name=name,
    )(*ins)


def pack_kernel(where, features, positions, vectors, filters, out):
    place, core = where[0], where[1]
    first = pl.multiple_of(core * 256, 256)
    turned = features[...].T
    chosen = lax.broadcasted_iota(jnp.int32, (32, WIDTH), 1) == (
        lax.broadcasted_iota(jnp.int32, (32, WIDTH), 0) * 16 + place
    )
    picked = lax.dot_general(
        chosen.astype(f32),
        filters[pl.ds(first, 256), :],
        NT,
        precision=lax.Precision.HIGHEST,
        preferred_element_type=f32,
    )
    own = vectors[:, pl.ds(first, 256)].astype(f32)
    coords = positions[...]
    for peer in range(16):
        out[peer, 0:FEATS, :] = turned[peer * FEATS : peer * FEATS + FEATS, :]
        out[peer, AT_POS : AT_POS + 3, :] = coords
        for half in range(2):
            lanes = slice(half * 128, half * 128 + 128)
            out[peer, AT_VEC + 3 * half : AT_VEC + 3 * half + 3, :] = own[:, lanes]
            out[peer, AT_FILTER + 2 * half : AT_FILTER + 2 * half + 2, :] = picked[
                2 * peer : 2 * peer + 2, lanes
            ]
        out[peer, ROWS - 3 : ROWS, :] = jnp.zeros((3, 128), f32)


def gather_filter_kernel(block, out, hot, rows):
    pair = lax.broadcasted_iota(jnp.int32, (128, 128), 0).astype(f32)
    row = lax.broadcasted_iota(jnp.int32, (32, 128), 0)
    third = (row // 2).astype(f32)
    odd = (row % 2) == 1
    for source in range(16):
        for half in range(2):
            at = AT_VEC + 3 * half
            n1 = block[source, at : at + 1, :]
            n2 = block[source, at + 1 : at + 2, :]
            n3 = block[source, at + 2 : at + 3, :]
            negative = (n1 < 0) | ((n1 == 0) & (n2 < 0))
            sign = jnp.where(negative, -1.0, 1.0)
            index = sign * (13.0 * n1 + n2)
            n3 = sign * n3
            index3 = jnp.where(n3 >= 0, n3, 8.0 - n3)
            lanes = slice((2 * source + half) * 128, (2 * source + half) * 128 + 128)
            hot[:, lanes] = (pair == index).astype(f32).astype(bf16)
            at = AT_FILTER + 2 * half
            value = jnp.where(odd, block[source, at + 1 : at + 2, :], block[source, at : at + 1, :])
            match = (third == index3).astype(f32)
            high, low = halves(match * value)
            rows[0:32, lanes] = high
            rows[32:64, lanes] = low
            rows[64:96, lanes] = match.astype(bf16)
    result = dot_nt(rows[...], hot[...])
    out[0:32, :] = result[0:32] + result[32:64]
    out[32:64, :] = result[64:96]


def forward_kernel(block, out, plane_high, plane_low, third_out, left):
    index = lax.broadcasted_iota(jnp.int32, (128, 128), 0).astype(f32)
    n1 = jnp.floor((index + 6.5) * (1.0 / 13.0))
    n2 = index - 13.0 * n1
    n3 = lax.broadcasted_iota(jnp.int32, (8, 128), 0).astype(f32)

    def tile(source, carry):
        lanes = pl.ds(pl.multiple_of(source * 128, 128), 128)
        first = block[source, AT_POS : AT_POS + 1, :]
        second = block[source, AT_POS + 1 : AT_POS + 2, :]
        last = block[source, AT_POS + 2 : AT_POS + 3, :]
        cosine, sine = turn(n1 * first + n2 * second)
        for at, value in ((0, cosine), (128, sine)):
            high, low = halves(value)
            plane_high[at : at + 128, lanes] = high
            plane_low[at : at + 128, lanes] = low
        third = jnp.concatenate(turn(n3 * last), axis=0)
        third_out[:, lanes] = third
        feats = block[source, 0:FEATS, :]
        for at, j in enumerate(USED):
            high, low = halves(third[j : j + 1, :] * feats)
            left[32 * at : 32 * at + 32, lanes] = high
            left[416 + 32 * at : 416 + 32 * at + 32, lanes] = low
        return carry

    lax.fori_loop(0, 16, tile, 0)
    both = dot_nt(left[...], plane_high[...])
    rest = dot_nt(left[0:416, :], plane_low[...])
    result = both[0:416] + (both[416:832] + rest)
    for j in (7, 8, 15):
        out[:, 2 * j : 2 * j + 2, :] = jnp.zeros((16, 2, 256), f32)
    for at, j in enumerate(USED):
        for side in range(2):
            start = 32 * at + 16 * side
            out[:, 2 * j + side, :] = result[start : start + 16, :]


def filter_kernel(parts, weights, out):
    total = parts[0]
    for source in range(1, 16):
        total = total + parts[source]
    cc, sc = total[0:16, 0:128], total[0:16, 128:256]
    cs, ss = total[16:32, 0:128], total[16:32, 128:256]
    plus, minus = weights[0:16, :], weights[16:32, :]
    plus_count, minus_count = weights[32:48, :], weights[48:64, :]
    cos_plus, cos_minus = cc - ss, cc + ss
    sin_plus, sin_minus = sc + cs, sc - cs
    energy = plus_count * (cos_plus * cos_plus + sin_plus * sin_plus)
    energy = energy + minus_count * (cos_minus * cos_minus + sin_minus * sin_minus)
    energy = jnp.sum(energy, axis=1, keepdims=True)
    odd = (lax.broadcasted_iota(jnp.int32, (16, 1), 0) % 2) == 1
    power_odd = jnp.sum(jnp.where(odd, energy, 0.0), axis=0, keepdims=True)
    power_even = jnp.sum(jnp.where(odd, 0.0, energy), axis=0, keepdims=True)
    power = jnp.where(odd, power_odd, power_even)
    scale = lax.rsqrt(power / (2 * KVEC) + epsilon) * (1.0 / 64.0)
    plus, minus = plus * scale, minus * scale
    cos_plus, cos_minus = plus * cos_plus, minus * cos_minus
    sin_plus, sin_minus = plus * sin_plus, minus * sin_minus
    upper = jnp.concatenate([cos_plus + cos_minus, sin_plus + sin_minus], axis=1)
    lower = jnp.concatenate([sin_plus - sin_minus, cos_minus - cos_plus], axis=1)
    both = jnp.concatenate([upper, lower], axis=0)
    for peer in range(16):
        out[peer] = both


def inverse_kernel(block, plane_high, plane_low, third, out, left):
    for at, j in enumerate(USED):
        for side in range(2):
            high, low = halves(block[:, 2 * j + side, :])
            start = 32 * at + 16 * side
            left[start : start + 16, :] = high
            left[416 + start : 416 + start + 16, :] = low

    def tile(step, carry):
        lanes = pl.ds(pl.multiple_of(step * 256, 256), 256)
        high = plane_high[:, lanes]
        both = dot(left[...], high)
        rest = dot(left[0:416, :], plane_low[:, lanes])
        basis = third[:, lanes]
        total = jnp.zeros((FEATS, 256), f32)
        for at, j in enumerate(USED):
            rows = slice(32 * at, 32 * at + 32)
            wide = both[rows] + (both[416 + 32 * at : 448 + 32 * at] + rest[rows])
            total = total + basis[j : j + 1, :] * wide
        out[2 * step] = total[:, 0:128]
        out[2 * step + 1] = total[:, 128:256]
        return carry

    lax.fori_loop(0, 8, tile, 0)


def short_kernel(
    before, own, after, slots, count, distance, w_self, w_neighbour, w_edge, w_message, out,
    left, right, total,
):
    nb_high, nb_low = halves(w_neighbour[...])
    for at, part in enumerate((before, own, after)):
        high, low = halves(part[...])
        projected = dot(high, nb_high) + (dot(high, nb_low) + dot(low, nb_high))
        left[:, at * 128 : at * 128 + 128] = (0.5 * projected).T.astype(bf16)
    edge_high, edge_low = halves(0.5 * w_edge[...])
    blank = jnp.zeros((80, WIDTH), f32)
    edges = jnp.concatenate(
        [edge_high.astype(f32), edge_low.astype(f32), edge_high.astype(f32), blank], axis=0
    )
    left[:, 384:512] = edges.T.astype(bf16)
    mine = (0.5 * dot3(own[...], w_self[...])).T
    right[432:512, :] = jnp.zeros((80, 256), bf16)
    total[...] = jnp.zeros_like(total)
    window = lax.broadcasted_iota(jnp.int32, (384, 128), 0)
    spacing = reach / (RADIAL - 1)
    centers = lax.broadcasted_iota(jnp.int32, (RADIAL, 128), 0).astype(f32) * spacing
    live = count[...]

    def step(pair, carry):
        for side in range(2):
            slot = 2 * pair + side
            lanes = slice(side * 128, side * 128 + 128)
            wanted = slots[pl.ds(slot, 1), :]
            right[0:384, lanes] = (window == wanted).astype(f32).astype(bf16)
            offset = (distance[pl.ds(slot, 1), :] - centers) / spacing
            high, low = halves(jnp.exp(-(offset * offset)))
            right[384:400, lanes] = high
            right[400:416, lanes] = high
            right[416:432, lanes] = low
        wide = dot(left[...], right[...])
        for side in range(2):
            half = wide[:, side * 128 : side * 128 + 128] + mine
            message = half + half * jnp.tanh(half)
            valid = (2 * pair + side < live).astype(f32)
            total[...] += message * valid
        return carry

    lax.fori_loop(0, SLOTS // 2, step, 0)
    summed = total[...].T * (1.0 / SLOTS)
    out[...] = own[...] + dot3(summed, w_message[...])


def update_kernel(block, base, gain, w_up, w_down, out):
    total = base[...] + block[...].reshape(WIDTH, 128).T
    mean = jnp.mean(total * total, axis=1, keepdims=True)
    normed = total * lax.rsqrt(mean + epsilon) * gain[...]
    hidden = dot3(normed, w_up[...])
    hidden = hidden * jax.nn.sigmoid(hidden)
    out[...] = total + dot3(hidden, w_down[...])


def local(
    features, positions, wavevectors, neighbour_slots, neighbour_count, pair_distance,
    w_self, w_neighbour, w_edge, w_message, spec_filter, norm_gain, w_up, w_down,
):
    devices = 1
    for axis in EVERY:
        devices *= lax.axis_size(axis)
    ahead = [(i, i + 1) for i in range(devices - 1)]
    place = lax.axis_index("x") * lax.axis_size("y") + lax.axis_index("y")
    where = jnp.stack([place, lax.axis_index("core")]).astype(jnp.int32)

    packed = call(
        pack_kernel, jax.ShapeDtypeStruct((16, ROWS, 128), f32),
        [where, features, positions, wavevectors, spec_filter], scalars=1, name="pack",
    )
    block = lax.all_to_all(packed, TRADE, 0, 0, tiled=True)
    block, ready = lax.optimization_barrier((block, features))
    before = lax.ppermute(ready, EVERY, ahead)
    after = lax.ppermute(ready, EVERY, [(t, s) for s, t in ahead])
    weights = call(
        gather_filter_kernel, jax.ShapeDtypeStruct((64, 128), f32), [block],
        scratch=[pltpu.VMEM((128, KVEC), bf16), pltpu.VMEM((96, KVEC), bf16)], name="weigh",
    )
    parts, plane_high, plane_low, third = call(
        forward_kernel,
        (
            jax.ShapeDtypeStruct((16, 32, 256), f32),
            jax.ShapeDtypeStruct((256, 2048), bf16),
            jax.ShapeDtypeStruct((256, 2048), bf16),
            jax.ShapeDtypeStruct((16, 2048), f32),
        ),
        [block], scratch=[pltpu.VMEM((832, 2048), bf16)], name="forward",
    )
    parts = lax.all_to_all(parts, TOTAL, 0, 0, tiled=True)
    filtered = call(
        filter_kernel, jax.ShapeDtypeStruct((16, 32, 256), f32), [parts, weights], name="filter",
    )
    filtered, before, after = lax.optimization_barrier((filtered, before, after))
    filtered = lax.all_to_all(filtered, TOTAL, 0, 0, tiled=True)
    beads = call(
        inverse_kernel, jax.ShapeDtypeStruct((16, FEATS, 128), f32),
        [filtered, plane_high, plane_low, third],
        scratch=[pltpu.VMEM((832, 256), bf16)], name="inverse",
    )
    beads = lax.all_to_all(beads, TRADE, 0, 0, tiled=True)
    base = call(
        short_kernel, jax.ShapeDtypeStruct((128, WIDTH), f32),
        [before, features, after, neighbour_slots, neighbour_count.reshape(1, 128), pair_distance,
         w_self, w_neighbour, w_edge, w_message],
        scratch=[
            pltpu.VMEM((WIDTH, 512), bf16),
            pltpu.VMEM((512, 256), bf16),
            pltpu.VMEM((WIDTH, 128), f32),
        ],
        flops=2 * 512 * 512 * 4096, name="short",
    )
    return call(
        update_kernel, jax.ShapeDtypeStruct((128, WIDTH), f32),
        [beads, base, norm_gain.reshape(1, WIDTH), w_up, w_down], name="update",
    )


def solution(mesh):
    fine = Mesh(mesh.devices.reshape(4, 4, 2, 4, 2), EVERY)
    placed = (
        P(EVERY, None),
        P(None, EVERY),
        P(None, ("zh", "zl")),
        P(None, EVERY),
        P(EVERY),
        P(None, EVERY),
        P(),
        P(),
        P(),
        P(),
        P(("zh", "zl"), None),
        P(),
        P(),
        P(),
    )
    return jax.shard_map(
        local, mesh=fine, in_specs=placed, out_specs=P(EVERY, None), check_vma=False
    )
```

profile of v0, /device:TPU:1, one launch (start us, length us, event | category | flops | bytes accessed | tf_op | source)
XLA Modules:
  0.0 96.8 jit_solution(14914014477913683926)
XLA Ops:
  0.0 0.6 pad_add_fusion.where
  0.6 2.7 %pack.1 = f32[16,48,128]{2,1,0:T(8,128)} custom-call(s32[2]{0:T(128)} %pad_add_fusion.where, f32[128,512]{1,0:T(8,128)} %own.1, f32[3,128]{1,0:T(4,128)} %positions.1, s32[3,512]{1,0:T(4,128)} %vectors.1, f32[512,512]{1,0:T(8,128)} %filters.1), custom_call_target="tpu_custom_call" | custom-call | bytes 1318408 | tf_op jit(solution)/shard_map/pack/pallas_call | solution.py:77
  3.3 22.5 %all_to_all.20.block = f32[16,48,128]{2,1,0:T(8,128)} all-to-all(f32[16,48,128]{2,1,0:T(8,128)} %pack.1), channel_id=1, replica_groups=mesh['x'=4,'y'=4,'core'=2,'zh'=4,'zl'=2] {'core','zh','zl'}, dimensions={0} | all-to-all | bytes 786432 | tf_op jit(solution)/shard_map/all_to_all | solution.py:309
  25.8 6.2 %forward.1 = (f32[16,32,256]{2,1,0:T(8,128)}, bf16[256,2048]{1,0:T(8,128)(2,1)}, bf16[256,2048]{1,0:T(8,128)(2,1)}, f32[16,2048]{1,0:T(8,128)}) custom-call(f32[16,48,128]{2,1,0:T(8,128)} %all_to_all.20.block), custom_call_target="tpu_custom_call" | custom-call | bytes 393216 | tf_op jit(solution)/shard_map/forward/pallas_call | solution.py:77
  32.0 6.9 %all-to-all-start.1 = ((f32[16,32,256]{2,1,0:T(8,128)}), f32[16,32,256]{2,1,0:T(8,128)S(1)}, u32[]{:S(2)}, u32[]{:S(2)}) async-start(f32[16,32,256]{2,1,0:T(8,128)} %get-tuple-element.15), calls=%async_computation.1 | async-start | bytes 1048576 | tf_op jit(solution)/shard_map/all_to_all | solution.py:327
  38.9 0.0 copy-done.2
  38.9 2.7 %collective-permute-start = (f32[128,512]{1,0:T(8,128)S(1)}, f32[128,512]{1,0:T(8,128)S(1)}, u32[]{:S(2)}, u32[]{:S(2)}) collective-permute-start(f32[128,512]{1,0:T(8,128)S(1)} %copy-done.2), channel_id=1, source_target_pairs={{0,1},{1,2},{2,3},{3,4},{4,5},{5,6},{6,7},{7,8},{8,9},{9,10},{10,1... | collective-permute-start | bytes 786440 | tf_op jit(solution)/shard_map/ppermute | solution.py:311
  41.6 4.1 %collective-permute-start.1 = (f32[128,512]{1,0:T(8,128)S(1)}, f32[128,512]{1,0:T(8,128)S(1)}, u32[]{:S(2)}, u32[]{:S(2)}) collective-permute-start(f32[128,512]{1,0:T(8,128)S(1)} %copy-done.2), channel_id=1, source_target_pairs={{1,0},{2,1},{3,2},{4,3},{5,4},{6,5},{7,6},{8,7},{9,8},{10,9},{11,1... | collective-permute-start | bytes 786440 | tf_op jit(solution)/shard_map/ppermute | solution.py:312
  45.7 2.4 %weigh.1.weights = f32[64,128]{1,0:T(8,128)} custom-call(f32[16,48,128]{2,1,0:T(8,128)} %all_to_all.20.block), custom_call_target="tpu_custom_call" | custom-call | bytes 393216 | tf_op jit(solution)/shard_map/weigh/pallas_call | solution.py:77
  48.1 1.0 %all-to-all-done.1.parts = f32[16,32,256]{2,1,0:T(8,128)S(1)} async-done(((f32[16,32,256]{2,1,0:T(8,128)}), f32[16,32,256]{2,1,0:T(8,128)S(1)}, u32[]{:S(2)}, u32[]{:S(2)}) %all-to-all-start.1) | async-done | bytes 524320 | tf_op jit(solution)/shard_map/all_to_all | solution.py:327
  49.1 0.8 copy-done
  49.9 2.0 %filter.1 = f32[16,32,256]{2,1,0:T(8,128)} custom-call(f32[16,32,256]{2,1,0:T(8,128)} %copy-done, f32[64,128]{1,0:T(8,128)} %weigh.1.weights), custom_call_target="tpu_custom_call" | custom-call | bytes 557056 | tf_op jit(solution)/shard_map/filter/pallas_call | solution.py:77
  51.9 0.0 collective-permute-done.before
  51.9 0.0 collective-permute-done.1.after
  51.9 0.0 copy-start.4
  52.0 14.9 %all_to_all.21.block = f32[16,32,256]{2,1,0:T(8,128)} all-to-all(f32[16,32,256]{2,1,0:T(8,128)} %filter.1), channel_id=1, replica_groups=mesh['x'=4,'y'=4,'core'=2,'zh'=4,'zl'=2] {'x','y'}, dimensions={0} | all-to-all | bytes 1048576 | tf_op jit(solution)/shard_map/all_to_all | solution.py:332
  66.9 0.0 copy-done.3
  66.9 0.0 copy-done.4
  66.9 6.4 %inverse.1 = f32[16,32,128]{2,1,0:T(8,128)} custom-call(f32[16,32,256]{2,1,0:T(8,128)} %all_to_all.21.block, bf16[256,2048]{1,0:T(8,128)(2,1)} %get-tuple-element.18.plane_high, bf16[256,2048]{1,0:T(8,128)(2,1)} %get-tuple-element.19.plane_low, f32[16,2048]{1,0:T(8,128)} %get-tuple-element.20.third), custom_call_target="tpu_custom_call" | custom-call | bytes 2752512 | tf_op jit(solution)/shard_map/inverse/pallas_call | solution.py:77
  73.3 9.2 %all-to-all-start.3 = ((f32[16,32,128]{2,1,0:T(8,128)}), f32[16,32,128]{2,1,0:T(8,128)S(1)}, u32[]{:S(2)}, u32[]{:S(2)}) async-start(f32[16,32,128]{2,1,0:T(8,128)} %inverse.1), calls=%async_computation.3 | async-start | bytes 524288 | tf_op jit(solution)/shard_map/all_to_all | solution.py:338
  82.4 10.3 %short.1.base = f32[128,512]{1,0:T(8,128)} custom-call(f32[128,512]{1,0:T(8,128)} %copy-done.3, f32[128,512]{1,0:T(8,128)} %own.1, f32[128,512]{1,0:T(8,128)} %copy-done.4, s32[32,128]{1,0:T(8,128)} %slots.1, s32[1,128]{1,0:T(1,128)} %bitcast.5, f32[32,128]{1,0:T(8,128)} %distance.1, f32[512,512]{1,0:T(8,128)} %w_self.1, f32[512,512]{1,0:T(8,128)} %w_neighbour.1, ...), custom_call_target="tpu_custom_call" | custom-call | flops 2147483648 | bytes 3998208 | tf_op jit(solution)/shard_map/short/pallas_call | solution.py:77
  92.8 0.0 all-to-all-done.3.block
  92.8 0.7 copy-done.1
  93.5 3.3 %update.1 = f32[128,512]{1,0:T(8,128)} custom-call(f32[16,32,128]{2,1,0:T(8,128)} %copy-done.1, f32[128,512]{1,0:T(8,128)} %short.1.base, f32[1,512]{1,0:T(1,128)} %bitcast.4, f32[512,512]{1,0:T(8,128)} %w_up.1, f32[512,512]{1,0:T(8,128)} %w_down.1), custom_call_target="tpu_custom_call" | custom-call | bytes 2623488 | tf_op jit(solution)/shard_map/update/pallas_call | solution.py:77
  (4 shorter events, 0.0 us)
Async XLA Ops:
  32.0 6.9 %copy-start.2 = (f32[128,512]{1,0:T(8,128)S(1)}, f32[128,512]{1,0:T(8,128)}, u32[]{:S(2)}) copy-start(f32[128,512]{1,0:T(8,128)} %own.1) | copy-start | bytes 786436
  32.0 17.2 %all-to-all-start.1 = ((f32[16,32,256]{2,1,0:T(8,128)}), f32[16,32,256]{2,1,0:T(8,128)S(1)}, u32[]{:S(2)}, u32[]{:S(2)}) async-start(f32[16,32,256]{2,1,0:T(8,128)} %get-tuple-element.15), calls=%async_computation.1 | async-start | bytes 1048576 | tf_op jit(solution)/shard_map/all_to_all | solution.py:327
  38.9 13.1 %collective-permute-start = (f32[128,512]{1,0:T(8,128)S(1)}, f32[128,512]{1,0:T(8,128)S(1)}, u32[]{:S(2)}, u32[]{:S(2)}) collective-permute-start(f32[128,512]{1,0:T(8,128)S(1)} %copy-done.2), channel_id=1, source_target_pairs={{0,1},{1,2},{2,3},{3,4},{4,5},{5,6},{6,7},{7,8},{8,9},{9,10},{10,1... | collective-permute-start | bytes 786440 | tf_op jit(solution)/shard_map/ppermute | solution.py:311
  41.6 10.4 %collective-permute-start.1 = (f32[128,512]{1,0:T(8,128)S(1)}, f32[128,512]{1,0:T(8,128)S(1)}, u32[]{:S(2)}, u32[]{:S(2)}) collective-permute-start(f32[128,512]{1,0:T(8,128)S(1)} %copy-done.2), channel_id=1, source_target_pairs={{1,0},{2,1},{3,2},{4,3},{5,4},{6,5},{7,6},{8,7},{9,8},{10,9},{11,1... | collective-permute-start | bytes 786440 | tf_op jit(solution)/shard_map/ppermute | solution.py:312
  49.1 0.8 copy-start
  51.9 14.9 %copy-start.3 = (f32[128,512]{1,0:T(8,128)}, f32[128,512]{1,0:T(8,128)S(1)}, u32[]{:S(2)}) copy-start(f32[128,512]{1,0:T(8,128)S(1)} %collective-permute-done.before) | copy-start | bytes 786436
  51.9 14.9 %copy-start.4 = (f32[128,512]{1,0:T(8,128)}, f32[128,512]{1,0:T(8,128)S(1)}, u32[]{:S(2)}) copy-start(f32[128,512]{1,0:T(8,128)S(1)} %collective-permute-done.1.after) | copy-start | bytes 786436
  73.3 19.5 %all-to-all-start.3 = ((f32[16,32,128]{2,1,0:T(8,128)}), f32[16,32,128]{2,1,0:T(8,128)S(1)}, u32[]{:S(2)}, u32[]{:S(2)}) async-start(f32[16,32,128]{2,1,0:T(8,128)} %inverse.1), calls=%async_computation.3 | async-start | bytes 524288 | tf_op jit(solution)/shard_map/all_to_all | solution.py:338
  92.8 0.7 copy-start.1
where the time goes:
time: 97.5 us; the launch traced here: 96.8 us
  blocking collectives  37.4 us (38%)
  Pallas kernels  33.3 us (34%)
  starting transfers between devices  22.8 us (23%)
  local copies, waits for them, and re-layouts  1.51 us (2%)
  waiting for transfers between devices  1.05 us (1%)
    pallas_call x7, Pallas kernels, call(): pl.pallas_call(kernel, out_shape=outs, in_specs=specs, out_specs=tuple(wh...  33.3 us
    all_to_all x1, blocking collectives, local(): block = lax.all_to_all(packed, TRADE, 0, 0, tiled=True)  22.5 us
    all_to_all x1, blocking collectives, local(): filtered = lax.all_to_all(filtered, TOTAL, 0, 0, tiled=True)  14.9 us
    all_to_all x1, starting transfers between devices, local(): beads = lax.all_to_all(beads, TRADE, 0, 0, tiled=True)  9.17 us
    all_to_all x1, starting transfers between devices, local(): parts = lax.all_to_all(parts, TOTAL, 0, 0, tiled=True)  6.89 us
    ppermute x1, starting transfers between devices, local(): after = lax.ppermute(ready, EVERY, [(t, s) for s, t in ahead])  4.07 us
    ppermute x1, starting transfers between devices, local(): before = lax.ppermute(ready, EVERY, ahead)  2.71 us
  transfers between devices with their start and end apart: 4, of which 1 were waited for; matrix products, arithmetic and copies ran while one was open for 0% of the time, Pallas kernels for 15%

commit v1 on v0

v1 whole, which is shorter than its diff:
```python
import jax
import jax.numpy as jnp
from jax import lax
from jax.experimental import pallas as pl
from jax.experimental.pallas import tpu as pltpu
from jax.sharding import Mesh, PartitionSpec as P


KVEC = 4096
WIDTH = 512
SLOTS = 32
RADIAL = 16
epsilon = 1e-05
reach = 2.5

TRADE = ("core", "zh", "zl")
TOTAL = ("x", "y")
EVERY = ("x", "y", "core", "zh", "zl")
FEATS = 32
AT_POS = 32
AT_VEC = 35
AT_FILTER = 41
ROWS = 48
USED = tuple(range(7)) + tuple(range(9, 15))

SIN = (6.283182792843448, -41.3414193330158, 81.59613740878913, -76.57967400034956,
       41.20368207513971, -12.268761447381701)
COS = (0.9999999890563522, -19.73920449855691, 64.93911741205494, -85.45013861232991,
       60.16762307755092, -25.967568454487537, 6.528613369793176)

bf16 = jnp.bfloat16
f32 = jnp.float32
NT = (((1,), (1,)), ((), ()))


def halves(value):
    high = value.astype(bf16)
    return high, (value - high.astype(f32)).astype(bf16)


def dot(left, right):
    return jnp.dot(left, right, preferred_element_type=f32)


def dot_nt(left, right):
    return lax.dot_general(left, right, NT, preferred_element_type=f32)


def dot3(left, right):
    left_high, left_low = halves(left)
    right_high, right_low = halves(right)
    return dot(left_high, right_high) + (dot(left_high, right_low) + dot(left_low, right_high))


def turn(cycles):
    part = cycles - jnp.round(cycles)
    square = part * part
    cosine = jnp.full_like(square, COS[-1])
    for factor in COS[-2::-1]:
        cosine = cosine * square + factor
    sine = jnp.full_like(square, SIN[-1])
    for factor in SIN[-2::-1]:
        sine = sine * square + factor
    return cosine, sine * part


class Held:
    def __init__(self, source, target, done):
        self.copy = pltpu.make_async_copy(source, target, done)
        self.target = target
        self.waiting = True
        self.copy.start()

    def get(self):
        if self.waiting:
            self.copy.wait()
            self.waiting = False
        return self.target


HBM = pltpu.HBM
VMEM = pltpu.VMEM


def call(kernel, outs, ins, mib, scratch=(), flops=0, copies=0):
    size = sum(v.size * v.dtype.itemsize for v, _ in ins)
    result = pl.pallas_call(
        kernel,
        out_shape=tuple(HBM(v.shape, v.dtype) if space is HBM else v for v, space in outs),
        in_specs=[pl.BlockSpec(memory_space=space) for _, space in ins],
        out_specs=tuple(pl.BlockSpec(memory_space=space) for _, space in outs),
        scratch_shapes=list(scratch) + [pltpu.SemaphoreType.DMA((copies,))] * (copies > 0),
        compiler_params=pltpu.CompilerParams(vmem_limit_bytes=mib * 1024 * 1024),
        cost_estimate=pl.CostEstimate(flops=flops, bytes_accessed=size, transcendentals=0),
    )(*[pltpu.with_memory_space_constraint(v, HBM) if space is HBM else v for v, space in ins])
    return result if len(outs) > 1 else result[0]


def pack_kernel(
    features, positions, vectors, filters, out, features_in, positions_in, vectors_in, filters_in,
    done,
):
    place = lax.axis_index("x") * 4 + lax.axis_index("y")
    first = pl.multiple_of(lax.axis_index("core") * 256, 256)
    filters = Held(filters.at[pl.ds(first, 256)], filters_in, done.at[0])
    features = Held(features, features_in, done.at[1])
    vectors = Held(vectors, vectors_in, done.at[2])
    positions = Held(positions, positions_in, done.at[3])
    chosen = lax.broadcasted_iota(jnp.int32, (32, WIDTH), 1) == (
        lax.broadcasted_iota(jnp.int32, (32, WIDTH), 0) * 16 + place
    )
    chosen = chosen.astype(f32).astype(bf16)
    high, low = halves(filters.get()[...])
    picked = dot_nt(chosen, high) + dot_nt(chosen, low)
    turned = features.get()[...].T
    own = vectors.get()[:, pl.ds(first, 256)].astype(f32)
    positions = positions.get()
    coords = positions[...]
    for peer in range(16):
        out[peer, 0:FEATS, :] = turned[peer * FEATS : peer * FEATS + FEATS, :]
        out[peer, AT_POS : AT_POS + 3, :] = coords
        for half in range(2):
            lanes = slice(half * 128, half * 128 + 128)
            out[peer, AT_VEC + 3 * half : AT_VEC + 3 * half + 3, :] = own[:, lanes]
            out[peer, AT_FILTER + 2 * half : AT_FILTER + 2 * half + 2, :] = picked[
                2 * peer : 2 * peer + 2, lanes
            ]
        out[peer, ROWS - 3 : ROWS, :] = jnp.zeros((3, 128), f32)


def weigh_kernel(block, out_far, third_far, hot, rows, out, third_out, done):
    number = lax.broadcasted_iota(jnp.int32, (8, 128), 0).astype(f32)
    for source in range(16):
        lanes = slice(source * 128, source * 128 + 128)
        cosine, sine = turn(number * block[source, AT_POS + 2 : AT_POS + 3, :])
        third_out[0:8, lanes] = cosine
        third_out[8:16, lanes] = sine
    third_copy = pltpu.make_async_copy(third_out, third_far, done.at[0])
    third_copy.start()
    pair = lax.broadcasted_iota(jnp.int32, (128, 128), 0).astype(f32)
    row = lax.broadcasted_iota(jnp.int32, (32, 128), 0)
    third = (row // 2).astype(f32)
    odd = (row % 2) == 1
    for source in range(16):
        for half in range(2):
            at = AT_VEC + 3 * half
            n1 = block[source, at : at + 1, :]
            n2 = block[source, at + 1 : at + 2, :]
            n3 = block[source, at + 2 : at + 3, :]
            negative = (n1 < 0) | ((n1 == 0) & (n2 < 0))
            sign = jnp.where(negative, -1.0, 1.0)
            n2 = sign * n2
            n3 = sign * n3
            index = 16.0 * (sign * n1) + jnp.where(n2 >= 0, n2, 8.0 - n2)
            index3 = jnp.where(n3 >= 0, n3, 8.0 - n3)
            lanes = slice((2 * source + half) * 128, (2 * source + half) * 128 + 128)
            hot[:, lanes] = (pair == index).astype(f32).astype(bf16)
            at = AT_FILTER + 2 * half
            value = jnp.where(odd, block[source, at + 1 : at + 2, :], block[source, at : at + 1, :])
            match = (third == index3).astype(f32)
            high, low = halves(match * value)
            rows[0:32, lanes] = high
            rows[32:64, lanes] = low
            rows[64:96, lanes] = match.astype(bf16)
    result = dot_nt(rows[...], hot[...])
    out[0:32, :] = result[0:32] + result[32:64]
    out[32:64, :] = result[64:96]
    copy = pltpu.make_async_copy(out, out_far, done.at[1])
    copy.start()
    third_copy.wait()
    copy.wait()


def forward_kernel(block, out_far, plane, left, out, done):
    number = lax.broadcasted_iota(jnp.int32, (8, 128), 0).astype(f32)
    blank = jnp.zeros((16, 2048), bf16)
    for at in range(112, 768, 128):
        plane[at : at + 16, :] = blank

    def tile(source, carry):
        lanes = pl.ds(pl.multiple_of(source * 128, 128), 128)
        cos1, sin1 = turn(number * block[source, AT_POS : AT_POS + 1, :])
        cos2, sin2 = turn(number * block[source, AT_POS + 1 : AT_POS + 2, :])
        cos3, sin3 = turn(number * block[source, AT_POS + 2 : AT_POS + 3, :])
        for n1 in range(7):
            cosine, sine = cos1[n1 : n1 + 1, :], sin1[n1 : n1 + 1, :]
            cc, ss = cosine * cos2, sine * sin2
            sc, cs = sine * cos2, cosine * sin2
            wave = jnp.concatenate([cc - ss, cc + ss], axis=0)
            high, low = halves(wave)
            at = 16 * n1
            plane[at : at + 16, lanes] = high
            plane[256 + at : 272 + at, lanes] = low
            plane[512 + at : 528 + at, lanes] = high
            wave = jnp.concatenate([sc + cs, sc - cs], axis=0)
            high, low = halves(wave)
            at = 128 + 16 * n1
            plane[at : at + 16, lanes] = high
            plane[256 + at : 272 + at, lanes] = low
            plane[512 + at : 528 + at, lanes] = high
        feats = block[source, 0:FEATS, :]
        for at, j in enumerate(USED):
            basis = cos3[j : j + 1, :] if j < 8 else sin3[j - 8 : j - 7, :]
            high, low = halves(basis * feats)
            left[32 * at : 32 * at + 32, lanes] = high
            left[416 + 32 * at : 416 + 32 * at + 32, lanes] = low
        return carry

    lax.fori_loop(0, 16, tile, 0, unroll=2)
    both = dot_nt(left[...], plane[0:256, :])
    rest = dot_nt(left[0:416, :], plane[256:512, :])
    result = both[0:416] + (both[416:832] + rest)
    for half in range(2):
        lanes = slice(128 * half, 128 * half + 128)
        for row in (14, 15, 16, 17, 30, 31):
            out[pl.ds(32 * half + row, 16, stride=64), :] = jnp.zeros((16, 128), f32)
        for at, j in enumerate(USED):
            for side in range(2):
                start = 32 * at + 16 * side
                rows = pl.ds(32 * half + 2 * j + side, 16, stride=64)
                out[rows, :] = result[start : start + 16, lanes]
    copy = pltpu.make_async_copy(out, out_far, done.at[0])
    copy.start()
    copy.wait()


def filter_kernel(parts_far, weights_far, out_far, parts, weights_in, out, done):
    fetches = [
        Held(parts_far.at[pl.ds(4 * i, 4)], parts.at[pl.ds(4 * i, 4)], done.at[i])
        for i in range(4)
    ]
    weights = Held(weights_far, weights_in, done.at[4])
    total = jnp.zeros((64, 128), f32)
    for i in range(4):
        fetches[i].get()
        for source in range(4 * i, 4 * i + 4):
            total = total + parts[source]
    weights = weights.get()
    cc, cs, sc, ss = total[0:16], total[16:32], total[32:48], total[48:64]
    plus, minus = weights[0:16, :], weights[16:32, :]
    plus_count, minus_count = weights[32:48, :], weights[48:64, :]
    cos_plus, cos_minus = cc - ss, cc + ss
    sin_plus, sin_minus = sc + cs, sc - cs
    energy = plus_count * (cos_plus * cos_plus + sin_plus * sin_plus)
    energy = energy + minus_count * (cos_minus * cos_minus + sin_minus * sin_minus)
    energy = jnp.sum(energy, axis=1, keepdims=True)
    odd = (lax.broadcasted_iota(jnp.int32, (16, 1), 0) % 2) == 1
    power_odd = jnp.sum(jnp.where(odd, energy, 0.0), axis=0, keepdims=True)
    power_even = jnp.sum(jnp.where(odd, 0.0, energy), axis=0, keepdims=True)
    power = jnp.where(odd, power_odd, power_even)
    scale = lax.rsqrt(power / (2 * KVEC) + epsilon) * (1.0 / 64.0)
    plus, minus = plus * scale, minus * scale
    cos_plus, cos_minus = plus * cos_plus, minus * cos_minus
    sin_plus, sin_minus = plus * sin_plus, minus * sin_minus
    out[0:16, :] = cos_plus + cos_minus
    out[16:32, :] = sin_plus - sin_minus
    out[32:48, :] = sin_plus + sin_minus
    out[48:64, :] = cos_minus - cos_plus
    copies = [
        pltpu.make_async_copy(out, out_far.at[peer], done.at[5 + peer]) for peer in range(16)
    ]
    for copy in copies:
        copy.start()
    for copy in copies:
        copy.wait()


def inverse_kernel(block_far, third_far, plane, out_far, left, block_in, third_in, out, done):
    block = Held(block_far, block_in, done.at[8])
    third = Held(third_far, third_in, done.at[9]).get()
    block = block.get()
    for at, j in enumerate(USED):
        for side in range(2):
            start = 32 * at + 16 * side
            for half in range(2):
                rows = pl.ds(32 * half + 2 * j + side, 16, stride=64)
                high, low = halves(block[rows, :])
                lane = 128 * half
                left[start : start + 16, lane : lane + 128] = high
                left[start : start + 16, 256 + lane : 384 + lane] = high
                left[start : start + 16, 512 + lane : 640 + lane] = low

    def send(step):
        rows = pl.ds(2 * step, 2)
        return pltpu.make_async_copy(out.at[rows], out_far.at[rows], done.at[step])

    def tile(step, carry):
        lanes = pl.ds(pl.multiple_of(step * 256, 256), 256)
        wide = dot(left[...], plane[:, lanes])
        basis = third[:, lanes]
        total = jnp.zeros((FEATS, 256), f32)
        for at, j in enumerate(USED):
            total = total + basis[j : j + 1, :] * wide[32 * at : 32 * at + 32]
        out[2 * step] = total[:, 0:128]
        out[2 * step + 1] = total[:, 128:256]
        send(step).start()
        return carry

    lax.fori_loop(0, 8, tile, 0, unroll=2)
    for step in range(8):
        send(step).wait()


def run_slots(low, high, slots, count, distance, left, mine, right, total):
    right[432:512, :] = jnp.zeros((80, 512), bf16)
    window = lax.broadcasted_iota(jnp.int32, (384, 128), 0)
    spacing = reach / (RADIAL - 1)
    centers = lax.broadcasted_iota(jnp.int32, (RADIAL, 128), 0).astype(f32) * spacing
    live = count[...]

    def step(quad, carry):
        for pair in range(2):
            for side in range(2):
                slot = 4 * quad + 2 * pair + side
                lanes = slice(256 * pair + side * 128, 256 * pair + side * 128 + 128)
                wanted = slots[pl.ds(slot, 1), :]
                hot = (window == wanted).astype(f32).astype(bf16)
                right[0:384, lanes] = hot
                right[512:896, lanes] = hot
                offset = (distance[pl.ds(slot, 1), :] - centers) / spacing
                upper, lower = halves(jnp.exp(-(offset * offset)))
                right[384:400, lanes] = upper
                right[400:416, lanes] = upper
                right[416:432, lanes] = lower
            wide = dot(left[...], right[:, 256 * pair : 256 * pair + 256])
            added = total[...]
            for side in range(2):
                half = wide[:, side * 128 : side * 128 + 128] + mine[...]
                message = half + half * jnp.tanh(half)
                valid = (4 * quad + 2 * pair + side < live).astype(f32)
                added = added + message * valid
            total[...] = added
        return carry

    lax.fori_loop(low, high, step, 0)


FIRST_QUADS = 2


def ready_kernel(
    before, own, after, w_self, w_neighbour, w_edge, slots, count, distance,
    left_far, mine_far, total_far,
    before_in, own_in, after_in, w_self_in, w_neighbour_in, w_edge_in, slots_in, count_in,
    distance_in, left, mine, total, right, done,
):
    w_neighbour = Held(w_neighbour, w_neighbour_in, done.at[0])
    parts = [
        Held(own, own_in, done.at[1]),
        Held(before, before_in, done.at[2]),
        Held(after, after_in, done.at[3]),
    ]
    w_self = Held(w_self, w_self_in, done.at[4])
    w_edge = Held(w_edge, w_edge_in, done.at[5])
    slots = Held(slots, slots_in, done.at[6])
    count = Held(count, count_in, done.at[7])
    distance = Held(distance, distance_in, done.at[8])
    nb_high, nb_low = halves(0.5 * w_neighbour.get()[...])
    for at, part in zip((128, 0, 256), parts):
        high, low = halves(part.get()[...])
        projected = dot(high, nb_high) + (dot(high, nb_low) + dot(low, nb_high))
        high, low = halves(projected.T)
        left[:, at : at + 128] = high
        left[:, 512 + at : 640 + at] = low
    edge_high, edge_low = halves(0.5 * w_edge.get()[...])
    edge_high, edge_low = edge_high.astype(f32), edge_low.astype(f32)
    blank = jnp.zeros((80, WIDTH), f32)
    edges = jnp.concatenate([edge_high, edge_low, edge_high, blank], axis=0)
    left[:, 384:512] = edges.T.astype(bf16)
    left_copy = pltpu.make_async_copy(left, left_far, done.at[9])
    left_copy.start()
    mine[...] = (0.5 * dot3(own_in[...], w_self.get()[...])).T
    mine_copy = pltpu.make_async_copy(mine, mine_far, done.at[10])
    mine_copy.start()
    total[...] = jnp.zeros_like(total)
    run_slots(
        0, FIRST_QUADS, slots.get(), count.get(), distance.get(), left, mine, right, total
    )
    total_copy = pltpu.make_async_copy(total, total_far, done.at[11])
    total_copy.start()
    left_copy.wait()
    mine_copy.wait()
    total_copy.wait()


def short_kernel(
    own, slots, count, distance, left, mine, total, w_message, out,
    own_in, slots_in, count_in, distance_in, left_in, mine_in, total_in, w_message_in, right, done,
):
    left = Held(left, left_in, done.at[0])
    slots = Held(slots, slots_in, done.at[1])
    count = Held(count, count_in, done.at[2])
    distance = Held(distance, distance_in, done.at[3])
    mine = Held(mine, mine_in, done.at[4])
    total = Held(total, total_in, done.at[5])
    w_message = Held(w_message, w_message_in, done.at[6])
    own = Held(own, own_in, done.at[7])
    run_slots(
        FIRST_QUADS, SLOTS // 4, slots.get(), count.get(), distance.get(), left.get(),
        mine.get(), right, total.get(),
    )
    summed = total_in[...].T * (1.0 / SLOTS)
    out[...] = own.get()[...] + dot3(summed, w_message.get()[...])


def update_kernel(block, base, gain, w_up, w_down, out):
    total = base[...] + block[...].reshape(WIDTH, 128).T
    mean = jnp.mean(total * total, axis=1, keepdims=True)
    normed = total * lax.rsqrt(mean + epsilon) * gain[...]
    hidden = dot3(normed, w_up[...])
    hidden = hidden * jax.nn.sigmoid(hidden)
    out[...] = total + dot3(hidden, w_down[...])


def swap(value, axes):
    return lax.all_to_all(value, axes, 0, 0, tiled=True)


def shape(*dims, dtype=f32):
    return jax.ShapeDtypeStruct(dims, dtype)


def local(
    features, positions, wavevectors, neighbour_slots, neighbour_count, pair_distance,
    w_self, w_neighbour, w_edge, w_message, spec_filter, norm_gain, w_up, w_down,
):
    devices = 1
    for axis in EVERY:
        devices *= lax.axis_size(axis)
    ahead = [(i, i + 1) for i in range(devices - 1)]

    packed = call(
        pack_kernel, [(shape(16, ROWS, 128), VMEM)],
        [(features, HBM), (positions, HBM), (wavevectors, HBM), (spec_filter, HBM)], 8,
        scratch=[
            VMEM((128, WIDTH), f32), VMEM((3, 128), f32), VMEM((3, 512), jnp.int32),
            VMEM((256, WIDTH), f32),
        ],
        copies=4,
    )
    block = swap(packed, TRADE)
    block, ready = lax.optimization_barrier((block, features))
    before = lax.ppermute(ready, EVERY, ahead)
    after = lax.ppermute(ready, EVERY, [(t, s) for s, t in ahead])
    parts, plane = call(
        forward_kernel,
        [(shape(1024, 128), HBM), (shape(768, 2048, dtype=bf16), VMEM)],
        [(block, VMEM)], 16,
        scratch=[VMEM((832, 2048), bf16), VMEM((1024, 128), f32)],
        flops=10**9, copies=1,
    )
    parts = swap(parts.reshape(16, 64, 128), TOTAL)
    weights, third = call(
        weigh_kernel, [(shape(64, 128), HBM), (shape(16, 2048), HBM)], [(block, VMEM)], 8,
        scratch=[
            VMEM((128, KVEC), bf16), VMEM((96, KVEC), bf16), VMEM((64, 128), f32),
            VMEM((16, 2048), f32),
        ],
        flops=10**9, copies=2,
    )
    filtered = call(
        filter_kernel, [(shape(16, 64, 128), HBM)], [(parts, HBM), (weights, HBM)], 4,
        scratch=[VMEM((16, 64, 128), f32), VMEM((64, 128), f32), VMEM((64, 128), f32)],
        copies=21,
    )
    filtered = swap(filtered, TOTAL)
    lists = [
        (neighbour_slots, HBM), (neighbour_count.reshape(1, 128), HBM), (pair_distance, HBM),
    ]
    lists_in = [VMEM((32, 128), jnp.int32), VMEM((1, 128), jnp.int32), VMEM((32, 128), f32)]
    left, mine, total = call(
        ready_kernel,
        [(shape(WIDTH, 896, dtype=bf16), HBM), (shape(WIDTH, 128), HBM),
         (shape(WIDTH, 128), HBM)],
        [(before, HBM), (features, HBM), (after, HBM), (w_self, HBM), (w_neighbour, HBM),
         (w_edge, HBM)] + lists, 16,
        scratch=[
            VMEM((128, WIDTH), f32), VMEM((128, WIDTH), f32), VMEM((128, WIDTH), f32),
            VMEM((WIDTH, WIDTH), f32), VMEM((WIDTH, WIDTH), f32), VMEM((RADIAL, WIDTH), f32),
        ] + lists_in + [
            VMEM((WIDTH, 896), bf16), VMEM((WIDTH, 128), f32), VMEM((WIDTH, 128), f32),
            VMEM((896, 512), bf16),
        ],
        flops=2 * 10**9, copies=12,
    )
    beads = call(
        inverse_kernel, [(shape(16, FEATS, 128), HBM)],
        [(filtered.reshape(1024, 128), HBM), (third, HBM), (plane, VMEM)], 8,
        scratch=[
            VMEM((416, 768), bf16), VMEM((1024, 128), f32), VMEM((16, 2048), f32),
            VMEM((16, FEATS, 128), f32),
        ],
        flops=10**9, copies=10,
    )
    beads = swap(beads, TRADE)
    base = call(
        short_kernel, [(shape(128, WIDTH), VMEM)],
        [(features, HBM)] + lists + [(left, HBM), (mine, HBM), (total, HBM), (w_message, HBM)],
        12,
        scratch=[VMEM((128, WIDTH), f32)] + lists_in + [
            VMEM((WIDTH, 896), bf16), VMEM((WIDTH, 128), f32), VMEM((WIDTH, 128), f32),
            VMEM((WIDTH, WIDTH), f32), VMEM((896, 512), bf16),
        ],
        flops=2 * 896 * 512 * 4096, copies=8,
    )
    return call(
        update_kernel, [(shape(128, WIDTH), VMEM)],
        [(beads, VMEM), (base, VMEM), (norm_gain.reshape(1, WIDTH), VMEM), (w_up, VMEM),
         (w_down, VMEM)], 12,
    )


def solution(mesh):
    fine = Mesh(mesh.devices.reshape(4, 4, 2, 4, 2), EVERY)
    placed = (
        P(EVERY, None),
        P(None, EVERY),
        P(None, ("zh", "zl")),
        P(None, EVERY),
        P(EVERY),
        P(None, EVERY),
        P(),
        P(),
        P(),
        P(),
        P(("zh", "zl"), None),
        P(),
        P(),
        P(),
    )

    return jax.shard_map(
        local, mesh=fine, in_specs=placed, out_specs=P(EVERY, None), check_vma=False
    )
```

time: 97.5 us -> 90 us (0.923)
  blocking collectives: 37.4 us -> 22.2 us
  waiting for transfers between devices: 1.05 us -> 10.2 us
  starting transfers between devices: 22.8 us -> 26.7 us
  Pallas kernels: 33.3 us -> 29.5 us
    all_to_all x2 -> x1, blocking collectives: 37.4 us -> 22.2 us  [swap(): return lax.all_to_all(value, axes, 0, 0, tiled=True)]
    all_to_all x2 -> x3, waiting for transfers between devices: 1.05 us -> 10.2 us  [swap(): return lax.all_to_all(value, axes, 0, 0, tiled=True)]
    pallas_call x7 -> x8, Pallas kernels: 33.3 us -> 29.5 us  [call(): pl.pallas_call(kernel, out_shape=tuple((HBM(v.shape, v.dtype) if space is...]
    all_to_all x2 -> x3, starting transfers between devices: 16.1 us -> 18.9 us  [swap(): return lax.all_to_all(value, axes, 0, 0, tiled=True)]
    ppermute x1, starting transfers between devices: 4.07 us -> 5.9 us  [local(): after = lax.ppermute(ready, EVERY, [(t, s) for s, t in ahead])]
  transfers between devices with their start and end apart: 4 -> 5, of which waited for: 1 -> 2; matrix products, arithmetic and copies ran while one was open for 0% -> 0% of each run, Pallas kernels for 15% -> 21%
where the time goes in v1:
time: 90 us; the launch traced here: 89.5 us
  Pallas kernels  29.5 us (33%)
  starting transfers between devices  26.7 us (30%)
  blocking collectives  22.2 us (25%)
  waiting for transfers between devices  10.2 us (11%)
    pallas_call x8, Pallas kernels, call(): pl.pallas_call(kernel, out_shape=tuple((HBM(v.shape, v.dtype) if space is...  29.5 us
    all_to_all x1, blocking collectives, swap(): return lax.all_to_all(value, axes, 0, 0, tiled=True)  22.2 us
    all_to_all x3, starting transfers between devices, swap(): return lax.all_to_all(value, axes, 0, 0, tiled=True)  18.9 us
    all_to_all x3, waiting for transfers between devices, swap(): return lax.all_to_all(value, axes, 0, 0, tiled=True)  10.2 us
    ppermute x1, starting transfers between devices, local(): after = lax.ppermute(ready, EVERY, [(t, s) for s, t in ahead])  5.9 us
    ppermute x1, starting transfers between devices, local(): before = lax.ppermute(ready, EVERY, ahead)  1.92 us
  transfers between devices with their start and end apart: 5, of which 2 were waited for; matrix products, arithmetic and copies ran while one was open for 0% of the time, Pallas kernels for 21%

profile of v1, /device:TPU:1, one launch (start us, length us, event | category | flops | bytes accessed | tf_op | source)
XLA Modules:
  0.0 89.5 jit_solution(15436943462107151418)
XLA Ops:
  0.0 1.5 %shard_map.136 = f32[16,48,128]{2,1,0:T(8,128)S(1)} custom-call(f32[128,512]{1,0:T(8,128)} %own.3, f32[3,128]{1,0:T(4,128)} %positions.1, s32[3,512]{1,0:T(4,128)} %vectors.1, f32[512,512]{1,0:T(8,128)} %filters.1), custom_call_target="tpu_custom_call" | custom-call | bytes 1318400 | tf_op jit(solution)/shard_map/pallas_call | solution.py:87
  1.5 22.2 %all_to_all.20.block = f32[16,48,128]{2,1,0:T(8,128)S(1)} all-to-all(f32[16,48,128]{2,1,0:T(8,128)S(1)} %shard_map.136), channel_id=1, replica_groups=mesh['x'=4,'y'=4,'core'=2,'zh'=4,'zl'=2] {'core','zh','zl'}, dimensions={0} | all-to-all | bytes 786432 | tf_op jit(solution)/shard_map/all_to_all | solution.py:416
  23.8 5.0 %shard_map.137 = (f32[1024,128]{1,0:T(8,128)}, bf16[768,2048]{1,0:T(8,128)(2,1)S(1)}) custom-call(f32[16,48,128]{2,1,0:T(8,128)S(1)} %all_to_all.20.block), custom_call_target="tpu_custom_call" | custom-call | flops 1000000000 | bytes 393216 | tf_op jit(solution)/shard_map/pallas_call | solution.py:87
  28.8 6.8 %all-to-all-start.1 = ((f32[16,64,128]{2,1,0:T(8,128)}), f32[16,64,128]{2,1,0:T(8,128)}, u32[]{:S(2)}, u32[]{:S(2)}) async-start(f32[16,64,128]{2,1,0:T(8,128)} %bitcast.5), calls=%async_computation.1 | async-start | bytes 1048576 | tf_op jit(solution)/shard_map/all_to_all | solution.py:416
  35.6 1.5 %shard_map.138 = (f32[64,128]{1,0:T(8,128)}, f32[16,2048]{1,0:T(8,128)}) custom-call(f32[16,48,128]{2,1,0:T(8,128)S(1)} %all_to_all.20.block), custom_call_target="tpu_custom_call" | custom-call | flops 1000000000 | bytes 393216 | tf_op jit(solution)/shard_map/pallas_call | solution.py:87
  37.1 8.8 %all-to-all-done.1.parts_far = f32[16,64,128]{2,1,0:T(8,128)} async-done(((f32[16,64,128]{2,1,0:T(8,128)}), f32[16,64,128]{2,1,0:T(8,128)}, u32[]{:S(2)}, u32[]{:S(2)}) %all-to-all-start.1) | async-done | bytes 524320 | tf_op jit(solution)/shard_map/all_to_all | solution.py:416
  46.0 2.2 %shard_map.139 = f32[16,64,128]{2,1,0:T(8,128)} custom-call(f32[16,64,128]{2,1,0:T(8,128)} %all-to-all-done.1.parts_far, f32[64,128]{1,0:T(8,128)} %get-tuple-element.16.weights_far), custom_call_target="tpu_custom_call" | custom-call | bytes 557056 | tf_op jit(solution)/shard_map/pallas_call | solution.py:87
  48.2 4.3 %all-to-all-start.2 = ((f32[16,64,128]{2,1,0:T(8,128)}), f32[16,64,128]{2,1,0:T(8,128)}, u32[]{:S(2)}, u32[]{:S(2)}) async-start(f32[16,64,128]{2,1,0:T(8,128)} %shard_map.139), calls=%async_computation.2 | async-start | bytes 1048576 | tf_op jit(solution)/shard_map/all_to_all | solution.py:416
  52.4 1.9 %collective-permute-start = (f32[128,512]{1,0:T(8,128)}, f32[128,512]{1,0:T(8,128)S(1)}, u32[]{:S(2)}, u32[]{:S(2)}) collective-permute-start(f32[128,512]{1,0:T(8,128)} %own.3), channel_id=1, source_target_pairs={{0,1},{1,2},{2,3},{3,4},{4,5},{5,6},{6,7},{7,8},{8,9},{9,10},{10,1... | collective-permute-start | bytes 786440 | tf_op jit(solution)/shard_map/ppermute | solution.py:443
  54.4 5.9 %collective-permute-start.1 = (f32[128,512]{1,0:T(8,128)}, f32[128,512]{1,0:T(8,128)}, u32[]{:S(2)}, u32[]{:S(2)}) collective-permute-start(f32[128,512]{1,0:T(8,128)} %own.3), channel_id=1, source_target_pairs={{1,0},{2,1},{3,2},{4,3},{5,4},{6,5},{7,6},{8,7},{9,8},{10,9},{11,1... | collective-permute-start | bytes 786440 | tf_op jit(solution)/shard_map/ppermute | solution.py:444
  60.3 1.3 %all-to-all-done.2 = f32[16,64,128]{2,1,0:T(8,128)} async-done(((f32[16,64,128]{2,1,0:T(8,128)}), f32[16,64,128]{2,1,0:T(8,128)}, u32[]{:S(2)}, u32[]{:S(2)}) %all-to-all-start.2) | async-done | bytes 524320 | tf_op jit(solution)/shard_map/all_to_all | solution.py:416
  61.6 4.2 %shard_map.140 = f32[16,32,128]{2,1,0:T(8,128)} custom-call(f32[1024,128]{1,0:T(8,128)} %bitcast.1.block_far, f32[16,2048]{1,0:T(8,128)} %get-tuple-element.17.third_far, bf16[768,2048]{1,0:T(8,128)(2,1)S(1)} %get-tuple-element.18.plane), custom_call_target="tpu_custom_call" | custom-call | flops 1000000000 | bytes 3801088 | tf_op jit(solution)/shard_map/pallas_call | solution.py:87
  65.8 7.8 %all-to-all-start.3 = ((f32[16,32,128]{2,1,0:T(8,128)}), f32[16,32,128]{2,1,0:T(8,128)S(1)}, u32[]{:S(2)}, u32[]{:S(2)}) async-start(f32[16,32,128]{2,1,0:T(8,128)} %shard_map.140), calls=%async_computation.3 | async-start | bytes 524288 | tf_op jit(solution)/shard_map/all_to_all | solution.py:416
  73.6 0.0 collective-permute-done.before
  73.6 0.0 copy-start.3
  73.6 0.0 collective-permute-done.1.after
  73.6 0.7 copy-done.3
  74.3 6.1 %shard_map.141 = (bf16[512,896]{1,0:T(8,128)(2,1)}, f32[512,128]{1,0:T(8,128)}, f32[512,128]{1,0:T(8,128)}) custom-call(f32[128,512]{1,0:T(8,128)} %copy-done.3, f32[128,512]{1,0:T(8,128)} %own.3, f32[128,512]{1,0:T(8,128)} %collective-permute-done.1.after, f32[512,512]{1,0:T(8,128)} %w_self.1, f32[512,512]{1,0:T(8,128)} %w_neighbour.1, f32[16,512]{1,0:T(8,128)} %w_edge.1, ...), custom_call_target="tpu_custom_call" | custom-call | flops 2000000000 | bytes 2949632 | tf_op jit(solution)/shard_map/pallas_call | solution.py:87
  80.4 0.0 copy-start
  80.4 0.0 copy-start.1
  80.4 0.0 copy-start.2
  80.5 7.4 %shard_map.142.base = f32[128,512]{1,0:T(8,128)S(1)} custom-call(f32[128,512]{1,0:T(8,128)} %own.3, s32[32,128]{1,0:T(8,128)} %slots.3, s32[1,128]{1,0:T(1,128)} %bitcast.7, f32[32,128]{1,0:T(8,128)} %distance.3, bf16[512,896]{1,0:T(8,128)(2,1)} %get-tuple-element.20.left, f32[512,128]{1,0:T(8,128)} %get-tuple-element.21.mine, ...), custom_call_target="tpu_custom_call" | custom-call | flops 3758096384 | bytes 2785792 | tf_op jit(solution)/shard_map/pallas_call | solution.py:87
  87.8 0.0 all-to-all-done.3.block
  87.9 1.6 %shard_map.143 = f32[128,512]{1,0:T(8,128)} custom-call(f32[16,32,128]{2,1,0:T(8,128)S(1)} %all-to-all-done.3.block, f32[128,512]{1,0:T(8,128)S(1)} %shard_map.142.base, f32[1,512]{1,0:T(1,128)S(1)} %bitcast.4, f32[512,512]{1,0:T(8,128)S(1)} %copy-done, f32[512,512]{1,0:T(8,128)S(1)} %copy-done.1), custom_call_target="tpu_custom_call" | custom-call | bytes 2623488 | tf_op jit(solution)/shard_map/pallas_call | solution.py:87
  (3 shorter events, 0.0 us)
Async XLA Ops:
  28.8 17.1 %all-to-all-start.1 = ((f32[16,64,128]{2,1,0:T(8,128)}), f32[16,64,128]{2,1,0:T(8,128)}, u32[]{:S(2)}, u32[]{:S(2)}) async-start(f32[16,64,128]{2,1,0:T(8,128)} %bitcast.5), calls=%async_computation.1 | async-start | bytes 1048576 | tf_op jit(solution)/shard_map/all_to_all | solution.py:416
  48.2 13.5 %all-to-all-start.2 = ((f32[16,64,128]{2,1,0:T(8,128)}), f32[16,64,128]{2,1,0:T(8,128)}, u32[]{:S(2)}, u32[]{:S(2)}) async-start(f32[16,64,128]{2,1,0:T(8,128)} %shard_map.139), calls=%async_computation.2 | async-start | bytes 1048576 | tf_op jit(solution)/shard_map/all_to_all | solution.py:416
  52.4 21.1 %collective-permute-start = (f32[128,512]{1,0:T(8,128)}, f32[128,512]{1,0:T(8,128)S(1)}, u32[]{:S(2)}, u32[]{:S(2)}) collective-permute-start(f32[128,512]{1,0:T(8,128)} %own.3), channel_id=1, source_target_pairs={{0,1},{1,2},{2,3},{3,4},{4,5},{5,6},{6,7},{7,8},{8,9},{9,10},{10,1... | collective-permute-start | bytes 786440 | tf_op jit(solution)/shard_map/ppermute | solution.py:443
  54.4 19.2 %collective-permute-start.1 = (f32[128,512]{1,0:T(8,128)}, f32[128,512]{1,0:T(8,128)}, u32[]{:S(2)}, u32[]{:S(2)}) collective-permute-start(f32[128,512]{1,0:T(8,128)} %own.3), channel_id=1, source_target_pairs={{1,0},{2,1},{3,2},{4,3},{5,4},{6,5},{7,6},{8,7},{9,8},{10,9},{11,1... | collective-permute-start | bytes 786440 | tf_op jit(solution)/shard_map/ppermute | solution.py:444
  65.8 22.0 %all-to-all-start.3 = ((f32[16,32,128]{2,1,0:T(8,128)}), f32[16,32,128]{2,1,0:T(8,128)S(1)}, u32[]{:S(2)}, u32[]{:S(2)}) async-start(f32[16,32,128]{2,1,0:T(8,128)} %shard_map.140), calls=%async_computation.3 | async-start | bytes 524288 | tf_op jit(solution)/shard_map/all_to_all | solution.py:416
  73.6 0.7 copy-start.3
  80.4 7.4 %copy-start = (f32[512,512]{1,0:T(8,128)S(1)}, f32[512,512]{1,0:T(8,128)}, u32[]{:S(2)}) copy-start(f32[512,512]{1,0:T(8,128)} %w_up.1) | copy-start | bytes 3145732
  80.4 7.4 %copy-start.1 = (f32[512,512]{1,0:T(8,128)S(1)}, f32[512,512]{1,0:T(8,128)}, u32[]{:S(2)}) copy-start(f32[512,512]{1,0:T(8,128)} %w_down.1) | copy-start | bytes 3145732
  80.4 7.4 %copy-start.2 = (f32[512]{0:T(512)S(1)}, f32[512]{0:T(512)}, u32[]{:S(2)}) copy-start(f32[512]{0:T(512)} %param.25) | copy-start | bytes 6148

commit v2 on v1

--- a/solution.py
+++ b/solution.py
@@ -21,6 +21,7 @@
 AT_VEC = 35
 AT_FILTER = 41
 ROWS = 48
+PART = 56
 USED = tuple(range(7)) + tuple(range(9, 15))
 
 SIN = (6.283182792843448, -41.3414193330158, 81.59613740878913, -76.57967400034956,
@@ -174,11 +175,11 @@
 def forward_kernel(block, out_far, plane, left, out, done):
     number = lax.broadcasted_iota(jnp.int32, (8, 128), 0).astype(f32)
     blank = jnp.zeros((16, 2048), bf16)
-    for at in range(112, 768, 128):
+    for at in range(112, 512, 128):
         plane[at : at + 16, :] = blank
 
-    def tile(source, carry):
-        lanes = pl.ds(pl.multiple_of(source * 128, 128), 128)
+    for source in range(16):
+        lanes = slice(source * 128, source * 128 + 128)
         cos1, sin1 = turn(number * block[source, AT_POS : AT_POS + 1, :])
         cos2, sin2 = turn(number * block[source, AT_POS + 1 : AT_POS + 2, :])
         cos3, sin3 = turn(number * block[source, AT_POS + 2 : AT_POS + 3, :])
@@ -191,52 +192,48 @@
             at = 16 * n1
             plane[at : at + 16, lanes] = high
             plane[256 + at : 272 + at, lanes] = low
-            plane[512 + at : 528 + at, lanes] = high
             wave = jnp.concatenate([sc + cs, sc - cs], axis=0)
             high, low = halves(wave)
             at = 128 + 16 * n1
             plane[at : at + 16, lanes] = high
             plane[256 + at : 272 + at, lanes] = low
-            plane[512 + at : 528 + at, lanes] = high
         feats = block[source, 0:FEATS, :]
         for at, j in enumerate(USED):
             basis = cos3[j : j + 1, :] if j < 8 else sin3[j - 8 : j - 7, :]
             high, low = halves(basis * feats)
             left[32 * at : 32 * at + 32, lanes] = high
             left[416 + 32 * at : 416 + 32 * at + 32, lanes] = low
-        return carry
-
-    lax.fori_loop(0, 16, tile, 0, unroll=2)
-    both = dot_nt(left[...], plane[0:256, :])
-    rest = dot_nt(left[0:416, :], plane[256:512, :])
-    result = both[0:416] + (both[416:832] + rest)
+
+    wide, tall = [], []
+    for chunk in range(8):
+        lanes = slice(chunk * 256, chunk * 256 + 256)
+        wide += [left[0:416, lanes], left[0:416, lanes], left[416:832, lanes]]
+        tall += [plane[0:256, lanes], plane[256:512, lanes], plane[0:256, lanes]]
+    result = dot_nt(jnp.concatenate(wide, axis=1), jnp.concatenate(tall, axis=1))
     for half in range(2):
         lanes = slice(128 * half, 128 * half + 128)
-        for row in (14, 15, 16, 17, 30, 31):
-            out[pl.ds(32 * half + row, 16, stride=64), :] = jnp.zeros((16, 128), f32)
+        for row in (52, 53):
+            out[pl.ds(2 * half + row, 16, stride=PART), :] = jnp.zeros((16, 128), f32)
         for at, j in enumerate(USED):
             for side in range(2):
                 start = 32 * at + 16 * side
-                rows = pl.ds(32 * half + 2 * j + side, 16, stride=64)
+                rows = pl.ds(26 * half + 2 * at + side, 16, stride=PART)
                 out[rows, :] = result[start : start + 16, lanes]
     copy = pltpu.make_async_copy(out, out_far, done.at[0])
     copy.start()
     copy.wait()
 
 
-def filter_kernel(parts_far, weights_far, out_far, parts, weights_in, out, done):
-    fetches = [
-        Held(parts_far.at[pl.ds(4 * i, 4)], parts.at[pl.ds(4 * i, 4)], done.at[i])
-        for i in range(4)
-    ]
-    weights = Held(weights_far, weights_in, done.at[4])
-    total = jnp.zeros((64, 128), f32)
-    for i in range(4):
-        fetches[i].get()
-        for source in range(4 * i, 4 * i + 4):
-            total = total + parts[source]
+def filter_kernel(parts, weights_far, out_far, weights_in, out, done):
+    weights = Held(weights_far, weights_in, done.at[16])
+    total = parts[0]
+    for source in range(1, 16):
+        total = total + parts[source]
     weights = weights.get()
-    cc, cs, sc, ss = total[0:16], total[16:32], total[32:48], total[48:64]
+    row = lax.broadcasted_iota(jnp.int32, (16, 128), 0)
+    cc, sc = total[0:16], total[26:42]
+    cs = jnp.where(row < 2, 0.0, total[12:28])
+    ss = jnp.where(row < 2, 0.0, total[38:54])
     plus, minus = weights[0:16, :], weights[16:32, :]
     plus_count, minus_count = weights[32:48, :], weights[48:64, :]
     cos_plus, cos_minus = cc - ss, cc + ss
@@ -252,12 +249,13 @@
     plus, minus = plus * scale, minus * scale
     cos_plus, cos_minus = plus * cos_plus, minus * cos_minus
     sin_plus, sin_minus = plus * sin_plus, minus * sin_minus
-    out[0:16, :] = cos_plus + cos_minus
-    out[16:32, :] = sin_plus - sin_minus
-    out[32:48, :] = sin_plus + sin_minus
-    out[48:64, :] = cos_minus - cos_plus
+    out[0:14, :] = (cos_plus + cos_minus)[0:14]
+    out[14:26, :] = (sin_plus - sin_minus)[2:14]
+    out[26:40, :] = (sin_plus + sin_minus)[0:14]
+    out[40:52, :] = (cos_minus - cos_plus)[2:14]
+    out[52:56, :] = jnp.zeros((4, 128), f32)
     copies = [
-        pltpu.make_async_copy(out, out_far.at[peer], done.at[5 + peer]) for peer in range(16)
+        pltpu.make_async_copy(out, out_far.at[peer], done.at[peer]) for peer in range(16)
     ]
     for copy in copies:
         copy.start()
@@ -265,20 +263,19 @@
         copy.wait()
 
 
-def inverse_kernel(block_far, third_far, plane, out_far, left, block_in, third_in, out, done):
-    block = Held(block_far, block_in, done.at[8])
-    third = Held(third_far, third_in, done.at[9]).get()
-    block = block.get()
+def inverse_kernel(block, third_far, plane, out_far, left, third_in, out, done):
+    third = Held(third_far, third_in, done.at[8])
     for at, j in enumerate(USED):
         for side in range(2):
             start = 32 * at + 16 * side
             for half in range(2):
-                rows = pl.ds(32 * half + 2 * j + side, 16, stride=64)
+                rows = pl.ds(26 * half + 2 * at + side, 16, stride=PART)
                 high, low = halves(block[rows, :])
                 lane = 128 * half
                 left[start : start + 16, lane : lane + 128] = high
-                left[start : start + 16, 256 + lane : 384 + lane] = high
-                left[start : start + 16, 512 + lane : 640 + lane] = low
+                left[start : start + 16, 256 + lane : 384 + lane] = low
+
+    third = third.get()
 
     def send(step):
         rows = pl.ds(2 * step, 2)
@@ -286,7 +283,11 @@
 
     def tile(step, carry):
         lanes = pl.ds(pl.multiple_of(step * 256, 256), 256)
-        wide = dot(left[...], plane[:, lanes])
+        upper, lower = plane[0:256, lanes], plane[256:512, lanes]
+        wide = dot(
+            jnp.concatenate([left[:, 0:256], left[:, 0:256], left[:, 256:512]], axis=1),
+            jnp.concatenate([upper, lower, upper], axis=0),
+        )
         basis = third[:, lanes]
         total = jnp.zeros((FEATS, 256), f32)
         for at, j in enumerate(USED):
@@ -296,7 +297,7 @@
         send(step).start()
         return carry
 
-    lax.fori_loop(0, 8, tile, 0, unroll=2)
+    lax.fori_loop(0, 8, tile, 0, unroll=8)
     for step in range(8):
         send(step).wait()
 
@@ -341,23 +342,19 @@
 def ready_kernel(
     before, own, after, w_self, w_neighbour, w_edge, slots, count, distance,
     left_far, mine_far, total_far,
-    before_in, own_in, after_in, w_self_in, w_neighbour_in, w_edge_in, slots_in, count_in,
+    own_in, w_self_in, w_neighbour_in, w_edge_in, slots_in, count_in,
     distance_in, left, mine, total, right, done,
 ):
     w_neighbour = Held(w_neighbour, w_neighbour_in, done.at[0])
-    parts = [
-        Held(own, own_in, done.at[1]),
-        Held(before, before_in, done.at[2]),
-        Held(after, after_in, done.at[3]),
-    ]
+    own = Held(own, own_in, done.at[1])
     w_self = Held(w_self, w_self_in, done.at[4])
     w_edge = Held(w_edge, w_edge_in, done.at[5])
     slots = Held(slots, slots_in, done.at[6])
     count = Held(count, count_in, done.at[7])
     distance = Held(distance, distance_in, done.at[8])
     nb_high, nb_low = halves(0.5 * w_neighbour.get()[...])
-    for at, part in zip((128, 0, 256), parts):
-        high, low = halves(part.get()[...])
+    for at, part in ((0, before), (256, after), (128, own.get())):
+        high, low = halves(part[...])
         projected = dot(high, nb_high) + (dot(high, nb_low) + dot(low, nb_high))
         high, low = halves(projected.T)
         left[:, at : at + 128] = high
@@ -444,12 +441,12 @@
     after = lax.ppermute(ready, EVERY, [(t, s) for s, t in ahead])
     parts, plane = call(
         forward_kernel,
-        [(shape(1024, 128), HBM), (shape(768, 2048, dtype=bf16), VMEM)],
+        [(shape(16 * PART, 128), HBM), (shape(512, 2048, dtype=bf16), VMEM)],
         [(block, VMEM)], 16,
-        scratch=[VMEM((832, 2048), bf16), VMEM((1024, 128), f32)],
+        scratch=[VMEM((832, 2048), bf16), VMEM((16 * PART, 128), f32)],
         flops=10**9, copies=1,
     )
-    parts = swap(parts.reshape(16, 64, 128), TOTAL)
+    parts = swap(parts.reshape(16, PART, 128), TOTAL)
     weights, third = call(
         weigh_kernel, [(shape(64, 128), HBM), (shape(16, 2048), HBM)], [(block, VMEM)], 8,
         scratch=[
@@ -459,9 +456,9 @@
         flops=10**9, copies=2,
     )
     filtered = call(
-        filter_kernel, [(shape(16, 64, 128), HBM)], [(parts, HBM), (weights, HBM)], 4,
-        scratch=[VMEM((16, 64, 128), f32), VMEM((64, 128), f32), VMEM((64, 128), f32)],
-        copies=21,
+        filter_kernel, [(shape(16, PART, 128), HBM)], [(parts, VMEM), (weights, HBM)], 4,
+        scratch=[VMEM((64, 128), f32), VMEM((PART, 128), f32)],
+        copies=17,
     )
     filtered = swap(filtered, TOTAL)
     lists = [
@@ -472,10 +469,10 @@
         ready_kernel,
         [(shape(WIDTH, 896, dtype=bf16), HBM), (shape(WIDTH, 128), HBM),
          (shape(WIDTH, 128), HBM)],
-        [(before, HBM), (features, HBM), (after, HBM), (w_self, HBM), (w_neighbour, HBM),
+        [(before, VMEM), (features, HBM), (after, VMEM), (w_self, HBM), (w_neighbour, HBM),
          (w_edge, HBM)] + lists, 16,
         scratch=[
-            VMEM((128, WIDTH), f32), VMEM((128, WIDTH), f32), VMEM((128, WIDTH), f32),
+            VMEM((128, WIDTH), f32),
             VMEM((WIDTH, WIDTH), f32), VMEM((WIDTH, WIDTH), f32), VMEM((RADIAL, WIDTH), f32),
         ] + lists_in + [
             VMEM((WIDTH, 896), bf16), VMEM((WIDTH, 128), f32), VMEM((WIDTH, 128), f32),
@@ -485,12 +482,12 @@
     )
     beads = call(
         inverse_kernel, [(shape(16, FEATS, 128), HBM)],
-        [(filtered.reshape(1024, 128), HBM), (third, HBM), (plane, VMEM)], 8,
+        [(filtered.reshape(16 * PART, 128), VMEM), (third, HBM), (plane, VMEM)], 8,
         scratch=[
-            VMEM((416, 768), bf16), VMEM((1024, 128), f32), VMEM((16, 2048), f32),
+            VMEM((416, 512), bf16), VMEM((16, 2048), f32),
             VMEM((16, FEATS, 128), f32),
         ],
-        flops=10**9, copies=10,
+        flops=10**9, copies=9,
     )
     beads = swap(beads, TRADE)
     base = call(

time: 90 us -> 83.7 us (0.930)
  Pallas kernels: 29.5 us -> 25.9 us
  waiting for transfers between devices: 10.2 us -> 7.85 us
    pallas_call x8, Pallas kernels: 29.5 us -> 25.9 us  [call(): pl.pallas_call(kernel, out_shape=tuple((HBM(v.shape, v.dtype) if space is...]
    all_to_all x3, waiting for transfers between devices: 10.2 us -> 7.85 us  [swap(): return lax.all_to_all(value, axes, 0, 0, tiled=True)]
where the time goes in v2:
time: 83.7 us; the launch traced here: 83.1 us
  starting transfers between devices  26.9 us (32%)
  Pallas kernels  25.9 us (31%)
  blocking collectives  22.2 us (27%)
  waiting for transfers between devices  7.85 us (9%)
    pallas_call x8, Pallas kernels, call(): pl.pallas_call(kernel, out_shape=tuple((HBM(v.shape, v.dtype) if space is...  25.9 us
    all_to_all x1, blocking collectives, swap(): return lax.all_to_all(value, axes, 0, 0, tiled=True)  22.2 us
    all_to_all x3, starting transfers between devices, swap(): return lax.all_to_all(value, axes, 0, 0, tiled=True)  18.9 us
    all_to_all x3, waiting for transfers between devices, swap(): return lax.all_to_all(value, axes, 0, 0, tiled=True)  7.85 us
    ppermute x1, starting transfers between devices, local(): after = lax.ppermute(ready, EVERY, [(t, s) for s, t in ahead])  5.8 us
    ppermute x1, starting transfers between devices, local(): before = lax.ppermute(ready, EVERY, ahead)  2.27 us
  transfers between devices with their start and end apart: 5, of which 2 were waited for; matrix products, arithmetic and copies ran while one was open for 0% of the time, Pallas kernels for 21%

profile of v2, /device:TPU:1, one launch (start us, length us, event | category | flops | bytes accessed | tf_op | source)
XLA Modules:
  0.0 83.1 jit_solution(6751915485503040916)
XLA Ops:
  0.0 1.5 %shard_map.136 = f32[16,48,128]{2,1,0:T(8,128)S(1)} custom-call(f32[128,512]{1,0:T(8,128)} %own.3, f32[3,128]{1,0:T(4,128)} %positions.1, s32[3,512]{1,0:T(4,128)} %vectors.1, f32[512,512]{1,0:T(8,128)} %filters.1), custom_call_target="tpu_custom_call" | custom-call | bytes 1318400 | tf_op jit(solution)/shard_map/pallas_call | solution.py:88
  1.5 22.2 %all_to_all.20.block = f32[16,48,128]{2,1,0:T(8,128)S(1)} all-to-all(f32[16,48,128]{2,1,0:T(8,128)S(1)} %shard_map.136), channel_id=1, replica_groups=mesh['x'=4,'y'=4,'core'=2,'zh'=4,'zl'=2] {'core','zh','zl'}, dimensions={0} | all-to-all | bytes 786432 | tf_op jit(solution)/shard_map/all_to_all | solution.py:413
  23.8 3.4 %shard_map.137 = (f32[896,128]{1,0:T(8,128)}, bf16[512,2048]{1,0:T(8,128)(2,1)S(1)}) custom-call(f32[16,48,128]{2,1,0:T(8,128)S(1)} %all_to_all.20.block), custom_call_target="tpu_custom_call" | custom-call | flops 1000000000 | bytes 393216 | tf_op jit(solution)/shard_map/pallas_call | solution.py:88
  27.2 6.8 %all-to-all-start.1 = ((f32[16,56,128]{2,1,0:T(8,128)}), f32[16,56,128]{2,1,0:T(8,128)S(1)}, u32[]{:S(2)}, u32[]{:S(2)}) async-start(f32[16,56,128]{2,1,0:T(8,128)} %bitcast.6), calls=%async_computation.1 | async-start | bytes 917504 | tf_op jit(solution)/shard_map/all_to_all | solution.py:413
  34.0 0.0 copy-start.3
  34.0 1.5 %shard_map.138 = (f32[64,128]{1,0:T(8,128)}, f32[16,2048]{1,0:T(8,128)}) custom-call(f32[16,48,128]{2,1,0:T(8,128)S(1)} %all_to_all.20.block), custom_call_target="tpu_custom_call" | custom-call | flops 1000000000 | bytes 393216 | tf_op jit(solution)/shard_map/pallas_call | solution.py:88
  35.5 7.1 %all-to-all-done.1.parts = f32[16,56,128]{2,1,0:T(8,128)S(1)} async-done(((f32[16,56,128]{2,1,0:T(8,128)}), f32[16,56,128]{2,1,0:T(8,128)S(1)}, u32[]{:S(2)}, u32[]{:S(2)}) %all-to-all-start.1) | async-done | bytes 458784 | tf_op jit(solution)/shard_map/all_to_all | solution.py:413
  42.6 1.8 %shard_map.139 = f32[16,56,128]{2,1,0:T(8,128)} custom-call(f32[16,56,128]{2,1,0:T(8,128)S(1)} %all-to-all-done.1.parts, f32[64,128]{1,0:T(8,128)} %get-tuple-element.16.weights_far), custom_call_target="tpu_custom_call" | custom-call | bytes 491520 | tf_op jit(solution)/shard_map/pallas_call | solution.py:88
  44.4 4.3 %all-to-all-start.2 = ((f32[16,56,128]{2,1,0:T(8,128)}), f32[16,56,128]{2,1,0:T(8,128)S(1)}, u32[]{:S(2)}, u32[]{:S(2)}) async-start(f32[16,56,128]{2,1,0:T(8,128)} %shard_map.139), calls=%async_computation.2 | async-start | bytes 917504 | tf_op jit(solution)/shard_map/all_to_all | solution.py:413
  48.7 2.3 %collective-permute-start = (f32[128,512]{1,0:T(8,128)S(1)}, f32[128,512]{1,0:T(8,128)S(1)}, u32[]{:S(2)}, u32[]{:S(2)}) collective-permute-start(f32[128,512]{1,0:T(8,128)S(1)} %copy-done.3), channel_id=1, source_target_pairs={{0,1},{1,2},{2,3},{3,4},{4,5},{5,6},{6,7},{7,8},{8,9},{9,10},{10,1... | collective-permute-start | bytes 786440 | tf_op jit(solution)/shard_map/ppermute | solution.py:440
  51.0 5.8 %collective-permute-start.1 = (f32[128,512]{1,0:T(8,128)S(1)}, f32[128,512]{1,0:T(8,128)S(1)}, u32[]{:S(2)}, u32[]{:S(2)}) collective-permute-start(f32[128,512]{1,0:T(8,128)S(1)} %copy-done.3), channel_id=1, source_target_pairs={{1,0},{2,1},{3,2},{4,3},{5,4},{6,5},{7,6},{8,7},{9,8},{10,9},{11,1... | collective-permute-start | bytes 786440 | tf_op jit(solution)/shard_map/ppermute | solution.py:441
  56.8 0.8 all-to-all-done.2
  57.5 3.1 %shard_map.140 = f32[16,32,128]{2,1,0:T(8,128)} custom-call(f32[896,128]{1,0:T(8,128)S(1)} %bitcast.4, f32[16,2048]{1,0:T(8,128)} %get-tuple-element.17.third_far, bf16[512,2048]{1,0:T(8,128)(2,1)S(1)} %get-tuple-element.18.plane), custom_call_target="tpu_custom_call" | custom-call | flops 1000000000 | bytes 2686976 | tf_op jit(solution)/shard_map/pallas_call | solution.py:88
  60.6 7.8 %all-to-all-start.3 = ((f32[16,32,128]{2,1,0:T(8,128)}), f32[16,32,128]{2,1,0:T(8,128)S(1)}, u32[]{:S(2)}, u32[]{:S(2)}) async-start(f32[16,32,128]{2,1,0:T(8,128)} %shard_map.140), calls=%async_computation.3 | async-start | bytes 524288 | tf_op jit(solution)/shard_map/all_to_all | solution.py:413
  68.5 0.0 collective-permute-done.before
  68.5 0.0 collective-permute-done.1.after
  68.5 5.6 %shard_map.141 = (bf16[512,896]{1,0:T(8,128)(2,1)}, f32[512,128]{1,0:T(8,128)}, f32[512,128]{1,0:T(8,128)}) custom-call(f32[128,512]{1,0:T(8,128)S(1)} %collective-permute-done.before, f32[128,512]{1,0:T(8,128)} %own.3, f32[128,512]{1,0:T(8,128)S(1)} %collective-permute-done.1.after, f32[512,512]{1,0:T(8,128)} %w_self.1, f32[512,512]{1,0:T(8,128)} %w_neighbour.1, ...), custom_call_target="tpu_custom_call" | custom-call | flops 2000000000 | bytes 2949632 | tf_op jit(solution)/shard_map/pallas_call | solution.py:88
  74.0 0.0 copy-start
  74.0 0.0 copy-start.1
  74.1 0.0 copy-start.2
  74.1 7.3 %shard_map.142.base = f32[128,512]{1,0:T(8,128)S(1)} custom-call(f32[128,512]{1,0:T(8,128)} %own.3, s32[32,128]{1,0:T(8,128)} %slots.3, s32[1,128]{1,0:T(1,128)} %bitcast.8, f32[32,128]{1,0:T(8,128)} %distance.3, bf16[512,896]{1,0:T(8,128)(2,1)} %get-tuple-element.20.left, f32[512,128]{1,0:T(8,128)} %get-tuple-element.21.mine, ...), custom_call_target="tpu_custom_call" | custom-call | flops 3758096384 | bytes 2785792 | tf_op jit(solution)/shard_map/pallas_call | solution.py:88
  81.4 0.0 all-to-all-done.3.block
  81.4 0.0 copy-done
  81.5 1.6 %shard_map.143 = f32[128,512]{1,0:T(8,128)} custom-call(f32[16,32,128]{2,1,0:T(8,128)S(1)} %all-to-all-done.3.block, f32[128,512]{1,0:T(8,128)S(1)} %shard_map.142.base, f32[1,512]{1,0:T(1,128)S(1)} %bitcast.5, f32[512,512]{1,0:T(8,128)S(1)} %copy-done, f32[512,512]{1,0:T(8,128)S(1)} %copy-done.1), custom_call_target="tpu_custom_call" | custom-call | bytes 2623488 | tf_op jit(solution)/shard_map/pallas_call | solution.py:88
  (3 shorter events, 0.0 us)
Async XLA Ops:
  27.2 15.4 %all-to-all-start.1 = ((f32[16,56,128]{2,1,0:T(8,128)}), f32[16,56,128]{2,1,0:T(8,128)S(1)}, u32[]{:S(2)}, u32[]{:S(2)}) async-start(f32[16,56,128]{2,1,0:T(8,128)} %bitcast.6), calls=%async_computation.1 | async-start | bytes 917504 | tf_op jit(solution)/shard_map/all_to_all | solution.py:413
  34.0 14.7 %copy-start.3 = (f32[128,512]{1,0:T(8,128)S(1)}, f32[128,512]{1,0:T(8,128)}, u32[]{:S(2)}) copy-start(f32[128,512]{1,0:T(8,128)} %own.3) | copy-start | bytes 786436
  44.4 13.1 %all-to-all-start.2 = ((f32[16,56,128]{2,1,0:T(8,128)}), f32[16,56,128]{2,1,0:T(8,128)S(1)}, u32[]{:S(2)}, u32[]{:S(2)}) async-start(f32[16,56,128]{2,1,0:T(8,128)} %shard_map.139), calls=%async_computation.2 | async-start | bytes 917504 | tf_op jit(solution)/shard_map/all_to_all | solution.py:413
  48.7 19.8 %collective-permute-start = (f32[128,512]{1,0:T(8,128)S(1)}, f32[128,512]{1,0:T(8,128)S(1)}, u32[]{:S(2)}, u32[]{:S(2)}) collective-permute-start(f32[128,512]{1,0:T(8,128)S(1)} %copy-done.3), channel_id=1, source_target_pairs={{0,1},{1,2},{2,3},{3,4},{4,5},{5,6},{6,7},{7,8},{8,9},{9,10},{10,1... | collective-permute-start | bytes 786440 | tf_op jit(solution)/shard_map/ppermute | solution.py:440
  51.0 17.5 %collective-permute-start.1 = (f32[128,512]{1,0:T(8,128)S(1)}, f32[128,512]{1,0:T(8,128)S(1)}, u32[]{:S(2)}, u32[]{:S(2)}) collective-permute-start(f32[128,512]{1,0:T(8,128)S(1)} %copy-done.3), channel_id=1, source_target_pairs={{1,0},{2,1},{3,2},{4,3},{5,4},{6,5},{7,6},{8,7},{9,8},{10,9},{11,1... | collective-permute-start | bytes 786440 | tf_op jit(solution)/shard_map/ppermute | solution.py:441
  60.6 20.8 %all-to-all-start.3 = ((f32[16,32,128]{2,1,0:T(8,128)}), f32[16,32,128]{2,1,0:T(8,128)S(1)}, u32[]{:S(2)}, u32[]{:S(2)}) async-start(f32[16,32,128]{2,1,0:T(8,128)} %shard_map.140), calls=%async_computation.3 | async-start | bytes 524288 | tf_op jit(solution)/shard_map/all_to_all | solution.py:413
  74.0 7.4 %copy-start = (f32[512,512]{1,0:T(8,128)S(1)}, f32[512,512]{1,0:T(8,128)}, u32[]{:S(2)}) copy-start(f32[512,512]{1,0:T(8,128)} %w_up.1) | copy-start | bytes 3145732
  74.0 7.4 %copy-start.1 = (f32[512,512]{1,0:T(8,128)S(1)}, f32[512,512]{1,0:T(8,128)}, u32[]{:S(2)}) copy-start(f32[512,512]{1,0:T(8,128)} %w_down.1) | copy-start | bytes 3145732
  74.1 7.4 %copy-start.2 = (f32[512]{0:T(512)S(1)}, f32[512]{0:T(512)}, u32[]{:S(2)}) copy-start(f32[512]{0:T(512)} %param.25) | copy-start | bytes 6148

commit v3 on v2

--- a/solution.py
+++ b/solution.py
@@ -340,7 +340,7 @@
 
 
 def ready_kernel(
-    before, own, after, w_self, w_neighbour, w_edge, slots, count, distance,
+    paired, own, other, w_self, w_neighbour, w_edge, slots, count, distance,
     left_far, mine_far, total_far,
     own_in, w_self_in, w_neighbour_in, w_edge_in, slots_in, count_in,
     distance_in, left, mine, total, right, done,
@@ -353,8 +353,11 @@
     count = Held(count, count_in, done.at[7])
     distance = Held(distance, distance_in, done.at[8])
     nb_high, nb_low = halves(0.5 * w_neighbour.get()[...])
-    for at, part in ((0, before), (256, after), (128, own.get())):
-        high, low = halves(part[...])
+    odd = jnp.full((128, WIDTH), lax.axis_index("zl"), jnp.int32) == 1
+    paired, other = paired[...], other[...]
+    before, after = jnp.where(odd, paired, other), jnp.where(odd, other, paired)
+    for at, part in ((0, before), (256, after), (128, own.get()[...])):
+        high, low = halves(part)
         projected = dot(high, nb_high) + (dot(high, nb_low) + dot(low, nb_high))
         high, low = halves(projected.T)
         left[:, at : at + 128] = high
@@ -424,7 +427,9 @@
     devices = 1
     for axis in EVERY:
         devices *= lax.axis_size(axis)
-    ahead = [(i, i + 1) for i in range(devices - 1)]
+    inner = [(i, i ^ 1) for i in range(devices)]
+    outer = [(i, i + 1) for i in range(1, devices - 1, 2)]
+    outer = outer + [(t, s) for s, t in outer]
 
     packed = call(
         pack_kernel, [(shape(16, ROWS, 128), VMEM)],
@@ -437,8 +442,8 @@
     )
     block = swap(packed, TRADE)
     block, ready = lax.optimization_barrier((block, features))
-    before = lax.ppermute(ready, EVERY, ahead)
-    after = lax.ppermute(ready, EVERY, [(t, s) for s, t in ahead])
+    paired = lax.ppermute(ready, EVERY, inner)
+    other = lax.ppermute(ready, EVERY, outer)
     parts, plane = call(
         forward_kernel,
         [(shape(16 * PART, 128), HBM), (shape(512, 2048, dtype=bf16), VMEM)],
@@ -469,7 +474,7 @@
         ready_kernel,
         [(shape(WIDTH, 896, dtype=bf16), HBM), (shape(WIDTH, 128), HBM),
          (shape(WIDTH, 128), HBM)],
-        [(before, VMEM), (features, HBM), (after, VMEM), (w_self, HBM), (w_neighbour, HBM),
+        [(paired, VMEM), (features, HBM), (other, VMEM), (w_self, HBM), (w_neighbour, HBM),
          (w_edge, HBM)] + lists, 16,
         scratch=[
             VMEM((128, WIDTH), f32),

time: 83.7 us -> 83.7 us (level)
  waiting for transfers between devices: 7.85 us -> 9.23 us
  starting transfers between devices: 26.9 us -> 25.6 us
    all_to_all x3, waiting for transfers between devices: 7.85 us -> 9.22 us  [swap(): return lax.all_to_all(value, axes, 0, 0, tiled=True)]
    ppermute x2, starting transfers between devices: 8.07 us -> 6.7 us  [the longest x1 6.25 us: local(): other = lax.ppermute(ready, EVERY, outer)]
where the time goes in v3:
time: 83.7 us; the launch traced here: 83.2 us
  Pallas kernels  25.9 us (31%)
  starting transfers between devices  25.6 us (31%)
  blocking collectives  22.2 us (27%)
  waiting for transfers between devices  9.23 us (11%)
    pallas_call x8, Pallas kernels, call(): pl.pallas_call(kernel, out_shape=tuple((HBM(v.shape, v.dtype) if space is...  25.9 us
    all_to_all x1, blocking collectives, swap(): return lax.all_to_all(value, axes, 0, 0, tiled=True)  22.2 us
    all_to_all x3, starting transfers between devices, swap(): return lax.all_to_all(value, axes, 0, 0, tiled=True)  18.9 us
    all_to_all x3, waiting for transfers between devices, swap(): return lax.all_to_all(value, axes, 0, 0, tiled=True)  9.22 us
    ppermute x1, starting transfers between devices, local(): other = lax.ppermute(ready, EVERY, outer)  6.25 us
  transfers between devices with their start and end apart: 5, of which 2 were waited for; matrix products, arithmetic and copies ran while one was open for 0% of the time, Pallas kernels for 21%

profile of v3, /device:TPU:1, one launch (start us, length us, event | category | flops | bytes accessed | tf_op | source)
XLA Modules:
  0.0 83.2 jit_solution(1207945705779626275)
XLA Ops:
  0.0 1.5 %shard_map.136 = f32[16,48,128]{2,1,0:T(8,128)S(1)} custom-call(f32[128,512]{1,0:T(8,128)} %own.3, f32[3,128]{1,0:T(4,128)} %positions.1, s32[3,512]{1,0:T(4,128)} %vectors.1, f32[512,512]{1,0:T(8,128)} %filters.1), custom_call_target="tpu_custom_call" | custom-call | bytes 1318400 | tf_op jit(solution)/shard_map/pallas_call | solution.py:88
  1.5 22.2 %all_to_all.20.block = f32[16,48,128]{2,1,0:T(8,128)S(1)} all-to-all(f32[16,48,128]{2,1,0:T(8,128)S(1)} %shard_map.136), channel_id=1, replica_groups=mesh['x'=4,'y'=4,'core'=2,'zh'=4,'zl'=2] {'core','zh','zl'}, dimensions={0} | all-to-all | bytes 786432 | tf_op jit(solution)/shard_map/all_to_all | solution.py:416
  23.8 3.4 %shard_map.137 = (f32[896,128]{1,0:T(8,128)}, bf16[512,2048]{1,0:T(8,128)(2,1)S(1)}) custom-call(f32[16,48,128]{2,1,0:T(8,128)S(1)} %all_to_all.20.block), custom_call_target="tpu_custom_call" | custom-call | flops 1000000000 | bytes 393216 | tf_op jit(solution)/shard_map/pallas_call | solution.py:88
  27.2 6.8 %all-to-all-start.1 = ((f32[16,56,128]{2,1,0:T(8,128)}), f32[16,56,128]{2,1,0:T(8,128)S(1)}, u32[]{:S(2)}, u32[]{:S(2)}) async-start(f32[16,56,128]{2,1,0:T(8,128)} %bitcast.6), calls=%async_computation.1 | async-start | bytes 917504 | tf_op jit(solution)/shard_map/all_to_all | solution.py:416
  34.0 0.0 copy-start.3
  34.0 1.5 %shard_map.138 = (f32[64,128]{1,0:T(8,128)}, f32[16,2048]{1,0:T(8,128)}) custom-call(f32[16,48,128]{2,1,0:T(8,128)S(1)} %all_to_all.20.block), custom_call_target="tpu_custom_call" | custom-call | flops 1000000000 | bytes 393216 | tf_op jit(solution)/shard_map/pallas_call | solution.py:88
  35.5 7.1 %all-to-all-done.1.parts = f32[16,56,128]{2,1,0:T(8,128)S(1)} async-done(((f32[16,56,128]{2,1,0:T(8,128)}), f32[16,56,128]{2,1,0:T(8,128)S(1)}, u32[]{:S(2)}, u32[]{:S(2)}) %all-to-all-start.1) | async-done | bytes 458784 | tf_op jit(solution)/shard_map/all_to_all | solution.py:416
  42.6 1.8 %shard_map.139 = f32[16,56,128]{2,1,0:T(8,128)} custom-call(f32[16,56,128]{2,1,0:T(8,128)S(1)} %all-to-all-done.1.parts, f32[64,128]{1,0:T(8,128)} %get-tuple-element.16.weights_far), custom_call_target="tpu_custom_call" | custom-call | bytes 491520 | tf_op jit(solution)/shard_map/pallas_call | solution.py:88
  44.4 4.3 %all-to-all-start.2 = ((f32[16,56,128]{2,1,0:T(8,128)}), f32[16,56,128]{2,1,0:T(8,128)S(1)}, u32[]{:S(2)}, u32[]{:S(2)}) async-start(f32[16,56,128]{2,1,0:T(8,128)} %shard_map.139), calls=%async_computation.2 | async-start | bytes 917504 | tf_op jit(solution)/shard_map/all_to_all | solution.py:416
  48.7 0.5 collective-permute-start
  49.1 6.3 %collective-permute-start.1 = (f32[128,512]{1,0:T(8,128)S(1)}, f32[128,512]{1,0:T(8,128)S(1)}, u32[]{:S(2)}, u32[]{:S(2)}) collective-permute-start(f32[128,512]{1,0:T(8,128)S(1)} %copy-done.3), channel_id=1, source_target_pairs={{1,2},{3,4},{5,6},{7,8},{9,10},{11,12},{13,14},{15,16},{17,18},{19... | collective-permute-start | bytes 786440 | tf_op jit(solution)/shard_map/ppermute | solution.py:446
  55.4 2.1 %all-to-all-done.2 = f32[16,56,128]{2,1,0:T(8,128)S(1)} async-done(((f32[16,56,128]{2,1,0:T(8,128)}), f32[16,56,128]{2,1,0:T(8,128)S(1)}, u32[]{:S(2)}, u32[]{:S(2)}) %all-to-all-start.2) | async-done | bytes 458784 | tf_op jit(solution)/shard_map/all_to_all | solution.py:416
  57.5 3.1 %shard_map.140 = f32[16,32,128]{2,1,0:T(8,128)} custom-call(f32[896,128]{1,0:T(8,128)S(1)} %bitcast.4, f32[16,2048]{1,0:T(8,128)} %get-tuple-element.17.third_far, bf16[512,2048]{1,0:T(8,128)(2,1)S(1)} %get-tuple-element.18.plane), custom_call_target="tpu_custom_call" | custom-call | flops 1000000000 | bytes 2686976 | tf_op jit(solution)/shard_map/pallas_call | solution.py:88
  60.6 7.8 %all-to-all-start.3 = ((f32[16,32,128]{2,1,0:T(8,128)}), f32[16,32,128]{2,1,0:T(8,128)S(1)}, u32[]{:S(2)}, u32[]{:S(2)}) async-start(f32[16,32,128]{2,1,0:T(8,128)} %shard_map.140), calls=%async_computation.3 | async-start | bytes 524288 | tf_op jit(solution)/shard_map/all_to_all | solution.py:416
  68.5 0.0 collective-permute-done.paired
  68.5 0.0 collective-permute-done.1.other
  68.5 5.6 %shard_map.141 = (bf16[512,896]{1,0:T(8,128)(2,1)}, f32[512,128]{1,0:T(8,128)}, f32[512,128]{1,0:T(8,128)}) custom-call(f32[128,512]{1,0:T(8,128)S(1)} %collective-permute-done.paired, f32[128,512]{1,0:T(8,128)} %own.3, f32[128,512]{1,0:T(8,128)S(1)} %collective-permute-done.1.other, f32[512,512]{1,0:T(8,128)} %w_self.1, f32[512,512]{1,0:T(8,128)} %w_neighbour.1, ...), custom_call_target="tpu_custom_call" | custom-call | flops 2000000000 | bytes 2949632 | tf_op jit(solution)/shard_map/pallas_call | solution.py:88
  74.1 0.0 copy-start
  74.1 0.0 copy-start.1
  74.1 0.0 copy-start.2
  74.1 7.4 %shard_map.142.base = f32[128,512]{1,0:T(8,128)S(1)} custom-call(f32[128,512]{1,0:T(8,128)} %own.3, s32[32,128]{1,0:T(8,128)} %slots.3, s32[1,128]{1,0:T(1,128)} %bitcast.8, f32[32,128]{1,0:T(8,128)} %distance.3, bf16[512,896]{1,0:T(8,128)(2,1)} %get-tuple-element.20.left, f32[512,128]{1,0:T(8,128)} %get-tuple-element.21.mine, ...), custom_call_target="tpu_custom_call" | custom-call | flops 3758096384 | bytes 2785792 | tf_op jit(solution)/shard_map/pallas_call | solution.py:88
  81.5 0.0 all-to-all-done.3.block
  81.5 0.0 copy-done
  81.5 1.6 %shard_map.143 = f32[128,512]{1,0:T(8,128)} custom-call(f32[16,32,128]{2,1,0:T(8,128)S(1)} %all-to-all-done.3.block, f32[128,512]{1,0:T(8,128)S(1)} %shard_map.142.base, f32[1,512]{1,0:T(1,128)S(1)} %bitcast.5, f32[512,512]{1,0:T(8,128)S(1)} %copy-done, f32[512,512]{1,0:T(8,128)S(1)} %copy-done.1), custom_call_target="tpu_custom_call" | custom-call | bytes 2623488 | tf_op jit(solution)/shard_map/pallas_call | solution.py:88
  (3 shorter events, 0.0 us)
Async XLA Ops:
  27.2 15.4 %all-to-all-start.1 = ((f32[16,56,128]{2,1,0:T(8,128)}), f32[16,56,128]{2,1,0:T(8,128)S(1)}, u32[]{:S(2)}, u32[]{:S(2)}) async-start(f32[16,56,128]{2,1,0:T(8,128)} %bitcast.6), calls=%async_computation.1 | async-start | bytes 917504 | tf_op jit(solution)/shard_map/all_to_all | solution.py:416
  34.0 14.7 %copy-start.3 = (f32[128,512]{1,0:T(8,128)S(1)}, f32[128,512]{1,0:T(8,128)}, u32[]{:S(2)}) copy-start(f32[128,512]{1,0:T(8,128)} %own.3) | copy-start | bytes 786436
  44.4 13.1 %all-to-all-start.2 = ((f32[16,56,128]{2,1,0:T(8,128)}), f32[16,56,128]{2,1,0:T(8,128)S(1)}, u32[]{:S(2)}, u32[]{:S(2)}) async-start(f32[16,56,128]{2,1,0:T(8,128)} %shard_map.139), calls=%async_computation.2 | async-start | bytes 917504 | tf_op jit(solution)/shard_map/all_to_all | solution.py:416
  48.7 19.8 %collective-permute-start = (f32[128,512]{1,0:T(8,128)S(1)}, f32[128,512]{1,0:T(8,128)S(1)}, u32[]{:S(2)}, u32[]{:S(2)}) collective-permute-start(f32[128,512]{1,0:T(8,128)S(1)} %copy-done.3), channel_id=1, source_target_pairs={{0,1},{1,0},{2,3},{3,2},{4,5},{5,4},{6,7},{7,6},{8,9},{9,8},{10,11... | collective-permute-start | bytes 786440 | tf_op jit(solution)/shard_map/ppermute | solution.py:445
  49.1 19.3 %collective-permute-start.1 = (f32[128,512]{1,0:T(8,128)S(1)}, f32[128,512]{1,0:T(8,128)S(1)}, u32[]{:S(2)}, u32[]{:S(2)}) collective-permute-start(f32[128,512]{1,0:T(8,128)S(1)} %copy-done.3), channel_id=1, source_target_pairs={{1,2},{3,4},{5,6},{7,8},{9,10},{11,12},{13,14},{15,16},{17,18},{19... | collective-permute-start | bytes 786440 | tf_op jit(solution)/shard_map/ppermute | solution.py:446
  60.6 20.9 %all-to-all-start.3 = ((f32[16,32,128]{2,1,0:T(8,128)}), f32[16,32,128]{2,1,0:T(8,128)S(1)}, u32[]{:S(2)}, u32[]{:S(2)}) async-start(f32[16,32,128]{2,1,0:T(8,128)} %shard_map.140), calls=%async_computation.3 | async-start | bytes 524288 | tf_op jit(solution)/shard_map/all_to_all | solution.py:416
  74.1 7.4 %copy-start = (f32[512,512]{1,0:T(8,128)S(1)}, f32[512,512]{1,0:T(8,128)}, u32[]{:S(2)}) copy-start(f32[512,512]{1,0:T(8,128)} %w_up.1) | copy-start | bytes 3145732
  74.1 7.4 %copy-start.1 = (f32[512,512]{1,0:T(8,128)S(1)}, f32[512,512]{1,0:T(8,128)}, u32[]{:S(2)}) copy-start(f32[512,512]{1,0:T(8,128)} %w_down.1) | copy-start | bytes 3145732
  74.1 7.4 %copy-start.2 = (f32[512]{0:T(512)S(1)}, f32[512]{0:T(512)}, u32[]{:S(2)}) copy-start(f32[512]{0:T(512)} %param.25) | copy-start | bytes 6148

commit v4 on v3

--- a/solution.py
+++ b/solution.py
@@ -103,22 +103,22 @@
 ):
     place = lax.axis_index("x") * 4 + lax.axis_index("y")
     first = pl.multiple_of(lax.axis_index("core") * 256, 256)
+    features = Held(features, features_in, done.at[1])
     filters = Held(filters.at[pl.ds(first, 256)], filters_in, done.at[0])
-    features = Held(features, features_in, done.at[1])
     vectors = Held(vectors, vectors_in, done.at[2])
     positions = Held(positions, positions_in, done.at[3])
+    turned = features.get()[...].T
+    for peer in range(16):
+        out[peer, 0:FEATS, :] = turned[peer * FEATS : peer * FEATS + FEATS, :]
     chosen = lax.broadcasted_iota(jnp.int32, (32, WIDTH), 1) == (
         lax.broadcasted_iota(jnp.int32, (32, WIDTH), 0) * 16 + place
     )
     chosen = chosen.astype(f32).astype(bf16)
+    own = vectors.get()[:, pl.ds(first, 256)].astype(f32)
+    coords = positions.get()[...]
     high, low = halves(filters.get()[...])
     picked = dot_nt(chosen, high) + dot_nt(chosen, low)
-    turned = features.get()[...].T
-    own = vectors.get()[:, pl.ds(first, 256)].astype(f32)
-    positions = positions.get()
-    coords = positions[...]
     for peer in range(16):
-        out[peer, 0:FEATS, :] = turned[peer * FEATS : peer * FEATS + FEATS, :]
         out[peer, AT_POS : AT_POS + 3, :] = coords
         for half in range(2):
             lanes = slice(half * 128, half * 128 + 128)
@@ -384,8 +384,9 @@
 
 
 def short_kernel(
-    own, slots, count, distance, left, mine, total, w_message, out,
-    own_in, slots_in, count_in, distance_in, left_in, mine_in, total_in, w_message_in, right, done,
+    own, slots, count, distance, left, mine, total, w_message, w_up, w_down, out, w_split,
+    own_in, slots_in, count_in, distance_in, left_in, mine_in, total_in, w_message_in, w_up_in,
+    w_down_in, right, done,
 ):
     left = Held(left, left_in, done.at[0])
     slots = Held(slots, slots_in, done.at[1])
@@ -395,21 +396,30 @@
     total = Held(total, total_in, done.at[5])
     w_message = Held(w_message, w_message_in, done.at[6])
     own = Held(own, own_in, done.at[7])
+    w_up = Held(w_up, w_up_in, done.at[8])
+    w_down = Held(w_down, w_down_in, done.at[9])
     run_slots(
         FIRST_QUADS, SLOTS // 4, slots.get(), count.get(), distance.get(), left.get(),
         mine.get(), right, total.get(),
     )
     summed = total_in[...].T * (1.0 / SLOTS)
     out[...] = own.get()[...] + dot3(summed, w_message.get()[...])
-
-
-def update_kernel(block, base, gain, w_up, w_down, out):
+    w_split[0], w_split[1] = halves(w_up.get()[...])
+    w_split[2], w_split[3] = halves(w_down.get()[...])
+
+
+def split_dot(left, high, low):
+    left_high, left_low = halves(left)
+    return dot(left_high, high) + (dot(left_high, low) + dot(left_low, high))
+
+
+def update_kernel(block, base, gain, weights, out):
     total = base[...] + block[...].reshape(WIDTH, 128).T
     mean = jnp.mean(total * total, axis=1, keepdims=True)
     normed = total * lax.rsqrt(mean + epsilon) * gain[...]
-    hidden = dot3(normed, w_up[...])
+    hidden = split_dot(normed, weights[0], weights[1])
     hidden = hidden * jax.nn.sigmoid(hidden)
-    out[...] = total + dot3(hidden, w_down[...])
+    out[...] = total + split_dot(hidden, weights[2], weights[3])
 
 
 def swap(value, axes):
@@ -495,20 +505,22 @@
         flops=10**9, copies=9,
     )
     beads = swap(beads, TRADE)
-    base = call(
-        short_kernel, [(shape(128, WIDTH), VMEM)],
-        [(features, HBM)] + lists + [(left, HBM), (mine, HBM), (total, HBM), (w_message, HBM)],
-        12,
+    base, weights = call(
+        short_kernel, [(shape(128, WIDTH), VMEM), (shape(4, WIDTH, WIDTH, dtype=bf16), VMEM)],
+        [(features, HBM)] + lists + [(left, HBM), (mine, HBM), (total, HBM), (w_message, HBM),
+                                     (w_up, HBM), (w_down, HBM)],
+        16,
         scratch=[VMEM((128, WIDTH), f32)] + lists_in + [
             VMEM((WIDTH, 896), bf16), VMEM((WIDTH, 128), f32), VMEM((WIDTH, 128), f32),
-            VMEM((WIDTH, WIDTH), f32), VMEM((896, 512), bf16),
+            VMEM((WIDTH, WIDTH), f32), VMEM((WIDTH, WIDTH), f32), VMEM((WIDTH, WIDTH), f32),
+            VMEM((896, 512), bf16),
         ],
-        flops=2 * 896 * 512 * 4096, copies=8,
+        flops=2 * 896 * 512 * 4096, copies=10,
     )
     return call(
         update_kernel, [(shape(128, WIDTH), VMEM)],
-        [(beads, VMEM), (base, VMEM), (norm_gain.reshape(1, WIDTH), VMEM), (w_up, VMEM),
-         (w_down, VMEM)], 12,
+        [(beads, VMEM), (base, VMEM), (norm_gain.reshape(1, WIDTH), VMEM), (weights, VMEM)],
+        8,
     )
 
 

time: 83.7 us -> 83.7 us (level)
  no operation moved by 1% of the time
where the time goes in v4:
time: 83.7 us; the launch traced here: 83.1 us
  Pallas kernels  26 us (31%)
  starting transfers between devices  25.6 us (31%)
  blocking collectives  22.2 us (27%)
  waiting for transfers between devices  9.24 us (11%)
    pallas_call x8, Pallas kernels, call(): pl.pallas_call(kernel, out_shape=tuple((HBM(v.shape, v.dtype) if space is...  26 us
    all_to_all x1, blocking collectives, swap(): return lax.all_to_all(value, axes, 0, 0, tiled=True)  22.2 us
    all_to_all x3, starting transfers between devices, swap(): return lax.all_to_all(value, axes, 0, 0, tiled=True)  18.9 us
    all_to_all x3, waiting for transfers between devices, swap(): return lax.all_to_all(value, axes, 0, 0, tiled=True)  9.24 us
    ppermute x1, starting transfers between devices, local(): other = lax.ppermute(ready, EVERY, outer)  6.25 us
  transfers between devices with their start and end apart: 5, of which 2 were waited for; matrix products, arithmetic and copies ran while one was open for 0% of the time, Pallas kernels for 21%

profile of v4, /device:TPU:1, one launch (start us, length us, event | category | flops | bytes accessed | tf_op | source)
XLA Modules:
  0.0 83.1 jit_solution(12828632277857746857)
XLA Ops:
  0.0 1.4 %shard_map.136 = f32[16,48,128]{2,1,0:T(8,128)S(1)} custom-call(f32[128,512]{1,0:T(8,128)} %own.3, f32[3,128]{1,0:T(4,128)} %positions.1, s32[3,512]{1,0:T(4,128)} %vectors.1, f32[512,512]{1,0:T(8,128)} %filters.1), custom_call_target="tpu_custom_call" | custom-call | bytes 1318400 | tf_op jit(solution)/shard_map/pallas_call | solution.py:88
  1.4 22.2 %all_to_all.20.block = f32[16,48,128]{2,1,0:T(8,128)S(1)} all-to-all(f32[16,48,128]{2,1,0:T(8,128)S(1)} %shard_map.136), channel_id=1, replica_groups=mesh['x'=4,'y'=4,'core'=2,'zh'=4,'zl'=2] {'core','zh','zl'}, dimensions={0} | all-to-all | bytes 786432 | tf_op jit(solution)/shard_map/all_to_all | solution.py:426
  23.7 3.4 %shard_map.137 = (f32[896,128]{1,0:T(8,128)}, bf16[512,2048]{1,0:T(8,128)(2,1)S(1)}) custom-call(f32[16,48,128]{2,1,0:T(8,128)S(1)} %all_to_all.20.block), custom_call_target="tpu_custom_call" | custom-call | flops 1000000000 | bytes 393216 | tf_op jit(solution)/shard_map/pallas_call | solution.py:88
  27.1 6.8 %all-to-all-start.1 = ((f32[16,56,128]{2,1,0:T(8,128)}), f32[16,56,128]{2,1,0:T(8,128)S(1)}, u32[]{:S(2)}, u32[]{:S(2)}) async-start(f32[16,56,128]{2,1,0:T(8,128)} %bitcast.6), calls=%async_computation.1 | async-start | bytes 917504 | tf_op jit(solution)/shard_map/all_to_all | solution.py:426
  33.9 0.0 copy-start.1
  33.9 1.5 %shard_map.138 = (f32[64,128]{1,0:T(8,128)}, f32[16,2048]{1,0:T(8,128)}) custom-call(f32[16,48,128]{2,1,0:T(8,128)S(1)} %all_to_all.20.block), custom_call_target="tpu_custom_call" | custom-call | flops 1000000000 | bytes 393216 | tf_op jit(solution)/shard_map/pallas_call | solution.py:88
  35.4 7.1 %all-to-all-done.1.parts = f32[16,56,128]{2,1,0:T(8,128)S(1)} async-done(((f32[16,56,128]{2,1,0:T(8,128)}), f32[16,56,128]{2,1,0:T(8,128)S(1)}, u32[]{:S(2)}, u32[]{:S(2)}) %all-to-all-start.1) | async-done | bytes 458784 | tf_op jit(solution)/shard_map/all_to_all | solution.py:426
  42.5 1.8 %shard_map.139 = f32[16,56,128]{2,1,0:T(8,128)} custom-call(f32[16,56,128]{2,1,0:T(8,128)S(1)} %all-to-all-done.1.parts, f32[64,128]{1,0:T(8,128)} %get-tuple-element.18.weights_far), custom_call_target="tpu_custom_call" | custom-call | bytes 491520 | tf_op jit(solution)/shard_map/pallas_call | solution.py:88
  44.3 4.3 %all-to-all-start.2 = ((f32[16,56,128]{2,1,0:T(8,128)}), f32[16,56,128]{2,1,0:T(8,128)S(1)}, u32[]{:S(2)}, u32[]{:S(2)}) async-start(f32[16,56,128]{2,1,0:T(8,128)} %shard_map.139), calls=%async_computation.2 | async-start | bytes 917504 | tf_op jit(solution)/shard_map/all_to_all | solution.py:426
  48.6 0.0 copy-done.1
  48.6 0.4 collective-permute-start
  49.1 6.2 %collective-permute-start.1 = (f32[128,512]{1,0:T(8,128)S(1)}, f32[128,512]{1,0:T(8,128)S(1)}, u32[]{:S(2)}, u32[]{:S(2)}) collective-permute-start(f32[128,512]{1,0:T(8,128)S(1)} %copy-done.1), channel_id=1, source_target_pairs={{1,2},{3,4},{5,6},{7,8},{9,10},{11,12},{13,14},{15,16},{17,18},{19... | collective-permute-start | bytes 786440 | tf_op jit(solution)/shard_map/ppermute | solution.py:456
  55.3 2.1 %all-to-all-done.2 = f32[16,56,128]{2,1,0:T(8,128)S(1)} async-done(((f32[16,56,128]{2,1,0:T(8,128)}), f32[16,56,128]{2,1,0:T(8,128)S(1)}, u32[]{:S(2)}, u32[]{:S(2)}) %all-to-all-start.2) | async-done | bytes 458784 | tf_op jit(solution)/shard_map/all_to_all | solution.py:426
  57.5 3.1 %shard_map.140 = f32[16,32,128]{2,1,0:T(8,128)} custom-call(f32[896,128]{1,0:T(8,128)S(1)} %bitcast.4, f32[16,2048]{1,0:T(8,128)} %get-tuple-element.19.third_far, bf16[512,2048]{1,0:T(8,128)(2,1)S(1)} %get-tuple-element.20.plane), custom_call_target="tpu_custom_call" | custom-call | flops 1000000000 | bytes 2686976 | tf_op jit(solution)/shard_map/pallas_call | solution.py:88
  60.6 7.8 %all-to-all-start.3 = ((f32[16,32,128]{2,1,0:T(8,128)}), f32[16,32,128]{2,1,0:T(8,128)S(1)}, u32[]{:S(2)}, u32[]{:S(2)}) async-start(f32[16,32,128]{2,1,0:T(8,128)} %shard_map.140), calls=%async_computation.3 | async-start | bytes 524288 | tf_op jit(solution)/shard_map/all_to_all | solution.py:426
  68.4 0.0 collective-permute-done.paired
  68.4 0.0 collective-permute-done.1.other
  68.4 5.6 %shard_map.141 = (bf16[512,896]{1,0:T(8,128)(2,1)}, f32[512,128]{1,0:T(8,128)}, f32[512,128]{1,0:T(8,128)}) custom-call(f32[128,512]{1,0:T(8,128)S(1)} %collective-permute-done.paired, f32[128,512]{1,0:T(8,128)} %own.3, f32[128,512]{1,0:T(8,128)S(1)} %collective-permute-done.1.other, f32[512,512]{1,0:T(8,128)} %w_self.1, f32[512,512]{1,0:T(8,128)} %w_neighbour.1, ...), custom_call_target="tpu_custom_call" | custom-call | flops 2000000000 | bytes 2949632 | tf_op jit(solution)/shard_map/pallas_call | solution.py:88
  74.0 0.0 copy-start
  74.0 7.5 %shard_map.142 = (f32[128,512]{1,0:T(8,128)S(1)}, bf16[4,512,512]{2,1,0:T(8,128)(2,1)S(1)}) custom-call(f32[128,512]{1,0:T(8,128)} %own.3, s32[32,128]{1,0:T(8,128)} %slots.3, s32[1,128]{1,0:T(1,128)} %bitcast.8, f32[32,128]{1,0:T(8,128)} %distance.3, bf16[512,896]{1,0:T(8,128)(2,1)} %get-tuple-element.22.left, f32[512,128]{1,0:T(8,128)} %get-tuple-element.23.mine, ...), custom_call_target="tpu_custom_call" | custom-call | flops 3758096384 | bytes 4882944 | tf_op jit(solution)/shard_map/pallas_call | solution.py:88
  81.5 0.0 all-to-all-done.3.block
  81.5 0.0 copy-done
  81.6 1.6 %shard_map.143 = f32[128,512]{1,0:T(8,128)} custom-call(f32[16,32,128]{2,1,0:T(8,128)S(1)} %all-to-all-done.3.block, f32[128,512]{1,0:T(8,128)S(1)} %get-tuple-element.25.base, f32[1,512]{1,0:T(1,128)S(1)} %bitcast.5, bf16[4,512,512]{2,1,0:T(8,128)(2,1)S(1)} %get-tuple-element.26.weights), custom_call_target="tpu_custom_call" | custom-call | bytes 2623488 | tf_op jit(solution)/shard_map/pallas_call | solution.py:88
Async XLA Ops:
  27.1 15.4 %all-to-all-start.1 = ((f32[16,56,128]{2,1,0:T(8,128)}), f32[16,56,128]{2,1,0:T(8,128)S(1)}, u32[]{:S(2)}, u32[]{:S(2)}) async-start(f32[16,56,128]{2,1,0:T(8,128)} %bitcast.6), calls=%async_computation.1 | async-start | bytes 917504 | tf_op jit(solution)/shard_map/all_to_all | solution.py:426
  33.9 14.7 %copy-start.1 = (f32[128,512]{1,0:T(8,128)S(1)}, f32[128,512]{1,0:T(8,128)}, u32[]{:S(2)}) copy-start(f32[128,512]{1,0:T(8,128)} %own.3) | copy-start | bytes 786436
  44.3 13.2 %all-to-all-start.2 = ((f32[16,56,128]{2,1,0:T(8,128)}), f32[16,56,128]{2,1,0:T(8,128)S(1)}, u32[]{:S(2)}, u32[]{:S(2)}) async-start(f32[16,56,128]{2,1,0:T(8,128)} %shard_map.139), calls=%async_computation.2 | async-start | bytes 917504 | tf_op jit(solution)/shard_map/all_to_all | solution.py:426
  48.6 19.8 %collective-permute-start = (f32[128,512]{1,0:T(8,128)S(1)}, f32[128,512]{1,0:T(8,128)S(1)}, u32[]{:S(2)}, u32[]{:S(2)}) collective-permute-start(f32[128,512]{1,0:T(8,128)S(1)} %copy-done.1), channel_id=1, source_target_pairs={{0,1},{1,0},{2,3},{3,2},{4,5},{5,4},{6,7},{7,6},{8,9},{9,8},{10,11... | collective-permute-start | bytes 786440 | tf_op jit(solution)/shard_map/ppermute | solution.py:455
  49.1 19.3 %collective-permute-start.1 = (f32[128,512]{1,0:T(8,128)S(1)}, f32[128,512]{1,0:T(8,128)S(1)}, u32[]{:S(2)}, u32[]{:S(2)}) collective-permute-start(f32[128,512]{1,0:T(8,128)S(1)} %copy-done.1), channel_id=1, source_target_pairs={{1,2},{3,4},{5,6},{7,8},{9,10},{11,12},{13,14},{15,16},{17,18},{19... | collective-permute-start | bytes 786440 | tf_op jit(solution)/shard_map/ppermute | solution.py:456
  60.6 21.0 %all-to-all-start.3 = ((f32[16,32,128]{2,1,0:T(8,128)}), f32[16,32,128]{2,1,0:T(8,128)S(1)}, u32[]{:S(2)}, u32[]{:S(2)}) async-start(f32[16,32,128]{2,1,0:T(8,128)} %shard_map.140), calls=%async_computation.3 | async-start | bytes 524288 | tf_op jit(solution)/shard_map/all_to_all | solution.py:426
  74.0 7.5 %copy-start = (f32[512]{0:T(512)S(1)}, f32[512]{0:T(512)}, u32[]{:S(2)}) copy-start(f32[512]{0:T(512)} %param.25) | copy-start | bytes 6148
